TPU v7x, 32 devices: a whole 2x2x4 slice. The times are simulated.
32 devices in a mesh: seq: 4 (over z), batch: 8 (over y, x, core).
Axes of the slice: x: 2, y: 2, z: 4, core: 2. Of those that a mesh axis runs over, the one named last changes fastest.
Arguments:
- queries: bfloat16 [8, 2048, 2048], P('batch', 'seq'), may hold values from -6 to 6
- keys: bfloat16 [8, 2048, 2048], P('batch', 'seq'), may hold values from -6 to 6
- values: bfloat16 [8, 2048, 2048], P('batch', 'seq'), may hold values from -6 to 6
- level_gain: float32 [8, 2048, 128], P('batch', 'seq'), may hold values from 0.004 to 0.06
- out_weight: bfloat16 [2048, 2048], P('batch'), may hold values from -0.125 to 0.125
- out_grad: bfloat16 [8, 2048, 2048], P('batch', 'seq'), may hold values from -6 to 6
Outputs:
- query_grad: bfloat16 [8, 2048, 2048], P('batch', 'seq')
- key_grad: bfloat16 [8, 2048, 2048], P('batch', 'seq')
- value_grad: bfloat16 [8, 2048, 2048], P('batch', 'seq')
- gain_grad: float32 [8, 2048, 128], P('batch', 'seq')
- weight_grad: float32 [2048, 2048], P(('seq', 'batch'))
All inputs are finite; a program needn't handle non-finite values.
Results may differ from a plain program's by a relative error of at most 0.0064.
Values may be sent and summed in bfloat16 or wider, within the bound.
No kernel may reach another device: no remote copies, remote signals or barrier semaphores. Data moves between devices by JAX's collectives and lax.ppermute only.
A program may use at most 192 MiB of HBM per device.

v0:
```python
import jax
import jax.numpy as jnp
import numpy as np
from jax import lax
from jax.sharding import PartitionSpec as P

H = 16
HD = 128
GROUP = 64
LEVELS = 8


def swapped(value, axis, stride):
    mask = 2**stride
    pairs = [(source, source ^ mask) for source in range(lax.axis_size(axis))]
    return lax.ppermute(value, axis, pairs)


def level_selects(seg_len):
    loc_bits = (seg_len // GROUP).bit_length() - 1
    position = np.arange(seg_len, dtype=np.int32)
    group_id = position // GROUP
    crossed = group_id[:, None] ^ group_id[None, :]
    level_id = np.zeros((seg_len, seg_len), np.int32)
    for shift_bit in range(loc_bits):
        level_id = level_id + (crossed >> shift_bit > 0).astype(np.int32)
    causal = position[None, :] <= position[:, None]
    return [
        jnp.asarray(((level_id == level_num) & causal).astype(np.float32), jnp.float32)
        for level_num in range(loc_bits + 1)
    ]


def local(queries, keys, values, level_gain, out_weight, out_grad):
    seg_len = queries.shape[1]
    width = queries.shape[2]
    score_scale = HD ** (-0.5)
    seq_count = lax.axis_size("seq")
    n_bits = seq_count.bit_length() - 1
    seg_index = lax.axis_index("seq")
    selects = level_selects(seg_len)
    loc_bits = len(selects) - 1
    grad_rows = out_grad[0]
    attn_grad = lax.dot_general(
        grad_rows,
        lax.all_gather(out_weight, "batch", axis=0, tiled=True),
        (((1,), (1,)), ((), ())),
        preferred_element_type=jnp.float32,
    ).astype(jnp.bfloat16)
    query_heads = queries[0].reshape(seg_len, H, HD)
    key_heads = keys[0].reshape(seg_len, H, HD)
    value_heads = values[0].reshape(seg_len, H, HD)
    grad_heads = attn_grad.reshape(seg_len, H, HD)
    gains = level_gain[0].reshape(seg_len, LEVELS, H)
    own_bits = [(seg_index >> level_bit & 1).astype(jnp.float32) for level_bit in range(n_bits)]
    states = jnp.einsum("thd,the->hde", key_heads, value_heads, preferred_element_type=jnp.float32)
    running = states
    far_list = []
    for level_bit in range(n_bits):
        received = swapped(running, "seq", level_bit)
        far_list.append(received * own_bits[level_bit])
        running = running + received
    far_stack = jnp.stack(far_list)
    far_half = far_stack.astype(jnp.bfloat16)
    scores = (
        jnp.einsum("thd,shd->hts", query_heads, key_heads, preferred_element_type=jnp.float32)
        * score_scale
    )
    weight_mask = jnp.zeros((H, seg_len, seg_len), jnp.float32)
    for level_num in range(loc_bits + 1):
        weight_mask = weight_mask + selects[level_num][None] * gains[:, level_num, :].T[:, :, None]
    probs = (scores * weight_mask).astype(jnp.bfloat16)
    intra = jnp.einsum("hts,shd->thd", probs, value_heads, preferred_element_type=jnp.float32)
    far_gain = jnp.transpose(gains[:, loc_bits + 1 : loc_bits + 1 + n_bits, :], (1, 0, 2))
    projected = (
        jnp.einsum("thd,bhde->bthe", query_heads, far_half, preferred_element_type=jnp.float32)
        * score_scale
    )
    cross = jnp.sum(far_gain[..., None] * projected, axis=0)
    attn = (intra + cross).reshape(seg_len, width).astype(jnp.bfloat16)
    weight_grad = lax.psum_scatter(
        lax.dot_general(
            attn, grad_rows, (((0,), (0,)), ((), ())), preferred_element_type=jnp.float32
        ),
        ("seq", "batch"),
        scatter_dimension=0,
        tiled=True,
    )
    prob_grad = jnp.einsum(
        "thd,shd->hts", grad_heads, value_heads, preferred_element_type=jnp.float32
    )
    grad_v_in = jnp.einsum("hts,thd->shd", probs, grad_heads, preferred_element_type=jnp.float32)
    energy = prob_grad * scores
    local_gain = jnp.stack(
        [jnp.sum(energy * sel_mat[None], axis=2).T for sel_mat in selects], axis=1
    )
    score_grad = (prob_grad * weight_mask).astype(jnp.bfloat16)
    grad_q_in = (
        jnp.einsum("hts,shd->thd", score_grad, key_heads, preferred_element_type=jnp.float32)
        * score_scale
    )
    grad_k_in = (
        jnp.einsum("hts,thd->shd", score_grad, query_heads, preferred_element_type=jnp.float32)
        * score_scale
    )
    weighted = (far_gain[..., None] * grad_heads[None]).astype(jnp.bfloat16)
    grad_q_far = (
        jnp.einsum("bthe,bhde->thd", weighted, far_half, preferred_element_type=jnp.float32)
        * score_scale
    )
    cross_gain = jnp.transpose(jnp.sum(projected * grad_heads[None], axis=3), (1, 0, 2))
    weighted_query = (far_gain[..., None] * query_heads[None]).astype(jnp.bfloat16)
    far_grad = (
        jnp.einsum("bthd,the->bhde", weighted_query, grad_heads, preferred_element_type=jnp.float32)
        * score_scale
    )
    far_grad = far_grad * jnp.stack(own_bits)[:, None, None, None]
    pending = far_grad
    state_grad = jnp.zeros((H, HD, HD), jnp.float32)
    for level_bit in range(n_bits):
        received = swapped(pending[level_bit:], "seq", level_bit)
        state_grad = state_grad + (1.0 - own_bits[level_bit]) * received[0]
        pending = jnp.concatenate(
            [pending[: level_bit + 1], pending[level_bit + 1 :] + received[1:]], axis=0
        )
    state_half = state_grad.astype(jnp.bfloat16)
    grad_k = grad_k_in + jnp.einsum(
        "she,hde->shd", value_heads, state_half, preferred_element_type=jnp.float32
    )
    grad_v = grad_v_in + jnp.einsum(
        "shd,hde->she", key_heads, state_half, preferred_element_type=jnp.float32
    )
    spare = LEVELS - loc_bits - 1 - n_bits
    gain_grad = jnp.concatenate(
        [local_gain, cross_gain, jnp.zeros((seg_len, spare, H), jnp.float32)], axis=1
    )
    query_grad = (grad_q_in + grad_q_far).reshape(seg_len, width).astype(jnp.bfloat16)
    key_grad = grad_k.reshape(seg_len, width).astype(jnp.bfloat16)
    value_grad = grad_v.reshape(seg_len, width).astype(jnp.bfloat16)
    return (
        query_grad[None],
        key_grad[None],
        value_grad[None],
        gain_grad.reshape(seg_len, LEVELS * H)[None],
        weight_grad,
    )


def solution(mesh):
    placed = (
        P("batch", "seq", None),
        P("batch", "seq", None),
        P("batch", "seq", None),
        P("batch", "seq", None),
        P("batch", None),
        P("batch", "seq", None),
    )
    return jax.shard_map(
        local,
        mesh=mesh,
        in_specs=placed,
        out_specs=(
            P("batch", "seq", None),
            P("batch", "seq", None),
            P("batch", "seq", None),
            P("batch", "seq", None),
            P(("seq", "batch"), None),
        ),
        check_vma=False,
    )
```

profile of v0, /device:TPU:1, one launch (start us, length us, event | category | flops | bytes accessed | tf_op | source)
XLA Modules:
  0.0 376.3 jit_solution(508636424131754177)
XLA Ops:
  8.0 3.9 %copy.123 = bf16[1,512,2048]{1,2,0:T(8,128)(2,1)} copy(bf16[1,512,2048]{2,1,0:T(8,128)(2,1)} %param.12) | data formatting | bytes 4194304 | tf_op jit(solution)/shard_map/reshape;squeeze | solution.py:52
  11.9 2.3 copy.124
  16.8 2.2 collective-permute-start
  20.1 21.8 %collective-permute-done = f32[16,128,128]{2,1,0:T(8,128)} collective-permute-done((f32[16,128,128]{2,1,0:T(8,128)S(1)}, f32[16,128,128]{2,1,0:T(8,128)}, u32[]{:S(2)}, u32[]{:S(2)}) %collective-permute-start) | collective-permute-done | bytes 1048608 | tf_op jit(solution)/shard_map/ppermute | solution.py:16
  42.0 2.5 fusion.33
  44.5 2.2 collective-permute-start.1
  46.7 2.3 copy.126
  50.5 8.2 %fusion.18 = f32[16,512,512]{1,2,0:T(8,128)} fusion(bf16[512,16,128]{2,1,0:T(8,128)(2,1)S(1)} %bitcast.122, bf16[512,16,128]{2,1,0:T(8,128)(2,1)S(1)} %bitcast.119), kind=kOutput, calls=%fused_computation.38 | convolution fusion | flops 1073741824 | bytes 20971520 | tf_op jit(solution)/shard_map/thd,shd->hts/dot_general | solution.py:66
  58.7 33.7 %collective-permute-done.1 = f32[16,128,128]{2,1,0:T(8,128)} collective-permute-done((f32[16,128,128]{2,1,0:T(8,128)}, f32[16,128,128]{2,1,0:T(8,128)}, u32[]{:S(2)}, u32[]{:S(2)}) %collective-permute-start.1) | collective-permute-done | bytes 1048608 | tf_op jit(solution)/shard_map/ppermute | solution.py:16
  93.8 8.1 %fusion.20 = bf16[64,8,16,128]{3,1,2,0:T(8,128)(2,1)S(1)} fusion(bf16[2048,2048]{1,0:T(8,128)(2,1)} %all-gather.2.cloned.1.call-done, bf16[1,512,2048]{2,1,0:T(8,128)(2,1)S(1)} %copy-done), kind=kOutput, calls=%fused_computation.40 | convolution fusion | flops 4296015872 | bytes 12582912 | tf_op jit(solution)/shard_map/dot_general | solution.py:44
  103.9 2.5 broadcast_multiply_fusion
  106.4 5.3 %copy.101 = f32[512,16,128]{0,2,1:T(8,128)} copy(f32[512,16,128]{2,1,0:T(8,128)} %broadcast_multiply_fusion) | data formatting | bytes 8388608 | tf_op jit(solution)/shard_map/mul | solution.py:111
  111.6 4.3 %copy.96 = bf16[512,16,128]{0,2,1:T(8,128)(2,1)} copy(bf16[512,16,128]{2,1,0:T(8,128)(2,1)} %bitcast.116) | data formatting | bytes 4194304 | tf_op jit(solution)/shard_map/reshape | solution.py:53
  116.0 6.8 %fusion.1 = (f32[512,16,128]{0,2,1:T(8,128)S(1)}, f32[2,512,16]{1,0,2:T(2,128)}) fusion(f32[2,512,16]{1,0,2:T(2,128)} %copy.105, f32[512,16,128]{0,2,1:T(8,128)} %copy.101, bf16[512,16,128,1]{2,1,0,3:T(8,128)(2,1)} %bitcast.123, bf16[1,16,128,128]{3,2,1,0:T(8,128)(2,1)S(1)} %fusion.34, bf16[1,16,128,128]{3,2,1,0:T(8,128)(2,1)} %get-tuple-element.29), kind=kOutput, calls=%fused_computation.11 | convolution fusion | flops 544718848 | bytes 11665408 | tf_op jit(solution)/shard_map/thd,bhde->bthe/dot_general | solution.py:76
  122.7 18.2 %multiply_multiply_fusion = (f32[16,512,512]{1,2,0:T(8,128)}, bf16[16,512,512]{1,2,0:T(8,128)(2,1)S(1)}, bf16[16,512,512]{1,2,0:T(8,128)(2,1)}) fusion(f32[16,512,512]{1,2,0:T(8,128)} %fusion.18, f32[16,512]{1,0:T(8,128)} %get-tuple-element.32, f32[512,512]{0,1:T(8,128)} %constant.30.clone, f32[16,512]{1,0:T(8,128)} %get-tuple-element.33, ...), kind=kOutput, calls=%fused_computation.7 | convolution fusion | flops 1128267776 | bytes 58851328 | tf_op jit(solution)/shard_map/thd,shd->hts/dot_general | solution.py:89
  144.1 8.2 %fusion.13 = f32[2048,2048]{1,0:T(8,128)} fusion(bf16[512,2048]{0,1:T(8,128)(2,1)S(1)} %bitcast.138, bf16[1,512,2048]{2,1,0:T(8,128)(2,1)S(1)} %copy-done), kind=kOutput, calls=%fused_computation.31 | convolution fusion | flops 4294967296 | bytes 20971520 | tf_op jit(solution)/shard_map/dot_general | solution.py:82
  156.0 5.8 %multiply_bitcast_fusion = f32[2,16,128,128]{2,3,0,1:T(8,128)} fusion(f32[512,16,128]{2,0,1:T(8,128)S(1)} %copy.90, f32[2,512,16]{1,0,2:T(2,128)S(1)} %copy.85, bf16[512,16,128,1]{2,1,0,3:T(8,128)(2,1)S(1)} %bitcast.117, f32[2]{0:T(128)S(1)} %maximum_multiply_fusion), kind=kOutput, calls=%fused_computation.35 | convolution fusion | flops 541589504 | bytes 8454152 | tf_op jit(solution)/shard_map/bthd,the->bhde/dot_general | solution.py:114
  163.0 9.2 %multiply_reduce_fusion = (f32[16,512]{1,0:T(8,128)S(1)}, f32[16,512]{1,0:T(8,128)S(1)}, f32[16,512]{1,0:T(8,128)S(1)}, f32[16,512]{1,0:T(8,128)S(1)}) fusion(f32[16,512,512]{1,2,0:T(8,128)} %get-tuple-element.26, f32[512,512]{0,1:T(8,128)S(1)} %copy-done.16, f32[512,512]{0,1:T(8,128)S(1)} %copy-done.19, f32[512,512]{0,1:T(8,128)S(1)} %copy-done.18, ...), kind=kLoop, calls=%fused_computation | loop fusion | flops 33521664 | bytes 21102592 | tf_op jit(solution)/shard_map/reduce_sum | solution.py:95
  175.5 6.0 %fusion.6 = f32[16,128,512,1]{2,1,0,3:T(8,128)S(1)} fusion(bf16[1,16,128,128]{3,2,1,0:T(8,128)(2,1)S(1)} %fusion.34, bf16[1,16,128,128]{3,2,1,0:T(8,128)(2,1)S(1)} %copy-done.15, f32[512,16,128]{2,0,1:T(8,128)S(1)} %copy.86, f32[2,512,16]{1,0,2:T(2,128)S(1)} %copy.85), kind=kOutput, calls=%fused_computation.22 | convolution fusion | flops 541589504 | bytes 9502720 | tf_op jit(solution)/shard_map/bthe,bhde->thd/dot_general | solution.py:108
  181.6 3.6 fusion.5
  185.2 3.9 %copy.106 = bf16[1,512,2048]{2,1,0:T(8,128)(2,1)} copy(bf16[1,512,2048]{1,2,0:T(8,128)(2,1)} %bitcast.135) | data formatting | bytes 4194304
  189.1 42.0 %collective-permute-done.2 = f32[2,16,128,128]{2,3,0,1:T(8,128)} collective-permute-done((f32[2,16,128,128]{2,3,0,1:T(8,128)}, f32[2,16,128,128]{2,3,0,1:T(8,128)}, u32[]{:S(2)}, u32[]{:S(2)}) %collective-permute-start.2) | collective-permute-done | bytes 2097184 | tf_op jit(solution)/shard_map/ppermute | solution.py:16
  231.1 2.8 slice_add_fusion
  233.9 3.0 collective-permute-start.3
  237.0 8.2 %fusion.36 = f32[16,128,512]{2,1,0:T(8,128)} fusion(bf16[512,16,128]{0,2,1:T(8,128)(2,1)S(1)} %copy-done.14, bf16[16,512,512]{1,2,0:T(8,128)(2,1)} %copy-done.10), kind=kOutput, calls=%fused_computation.66 | convolution fusion | flops 1073741824 | bytes 14680064 | tf_op jit(solution)/shard_map/hts,thd->shd/dot_general | solution.py:92
  245.2 4.9 %fusion.16 = f32[16,512,128]{1,2,0:T(8,128)} fusion(bf16[16,512,512]{1,2,0:T(8,128)(2,1)S(1)} %bitcast.128, bf16[512,16,128]{2,1,0:T(8,128)(2,1)S(1)} %bitcast.124), kind=kOutput, calls=%fused_computation.36 | convolution fusion | flops 1073741824 | bytes 14680064 | tf_op jit(solution)/shard_map/hts,thd->shd/dot_general | solution.py:103
  250.1 43.2 %collective-permute-done.3 = f32[1,16,128,128]{2,3,0,1:T(8,128)} collective-permute-done((f32[1,16,128,128]{2,3,0,1:T(8,128)}, f32[1,16,128,128]{2,3,0,1:T(8,128)}, u32[]{:S(2)}, u32[]{:S(2)}) %collective-permute-start.3) | collective-permute-done | bytes 1048608 | tf_op jit(solution)/shard_map/ppermute | solution.py:16
  295.1 4.9 %add_convert_fusion = bf16[16,128,512]{2,1,0:T(8,128)(2,1)} fusion(f32[16,128,512]{2,1,0:T(8,128)} %fusion.36, bf16[16,128,128]{1,2,0:T(8,128)(2,1)S(1)} %fusion.35, bf16[512,16,128]{2,1,0:T(8,128)(2,1)S(1)} %bitcast.121), kind=kOutput, calls=%fused_computation.24 | convolution fusion | flops 270532608 | bytes 8912896 | tf_op jit(solution)/shard_map/shd,hde->she/dot_general | solution.py:130
  300.0 3.9 %copy.108 = bf16[1,512,2048]{2,1,0:T(8,128)(2,1)} copy(bf16[1,512,2048]{1,2,0:T(8,128)(2,1)} %bitcast.134) | data formatting | bytes 4194304
  303.9 5.1 %fusion.4 = bf16[512,16,128]{0,2,1:T(8,128)(2,1)} fusion(f32[16,512,128]{1,2,0:T(8,128)} %fusion.16, bf16[16,128,128]{1,2,0:T(8,128)(2,1)S(1)} %fusion.35, bf16[512,16,128]{0,2,1:T(8,128)(2,1)} %bitcast.129), kind=kOutput, calls=%fused_computation.18 | convolution fusion | flops 271581184 | bytes 8912896 | tf_op jit(solution)/shard_map/she,hde->shd/dot_general | solution.py:127
  309.0 3.9 %copy.107 = bf16[1,512,2048]{2,1,0:T(8,128)(2,1)} copy(bf16[1,512,2048]{1,2,0:T(8,128)(2,1)} %bitcast.133) | data formatting | bytes 4194304
  312.9 56.5 %reduce-scatter.2.cloned.1.call-done = f32[64,2048]{1,0:T(8,128)} async-done(((f32[2048,2048]{1,0:T(8,128)}), f32[64,2048]{1,0:T(8,128)}) %reduce-scatter.2.cloned.1.call-update) | async-done | bytes 524304 | tf_op jit(solution)/shard_map/reduce_scatter | solution.py:81
  (84 shorter events, 22.2 us)
Async XLA Ops:
  7.2 86.6 %copy-start = (bf16[1,512,2048]{2,1,0:T(8,128)(2,1)S(1)}, bf16[1,512,2048]{2,1,0:T(8,128)(2,1)}, u32[]{:S(2)}) copy-start(bf16[1,512,2048]{2,1,0:T(8,128)(2,1)} %param.15) | copy-start | bytes 6291460
  7.2 86.6 %all-gather.2.cloned.1.call-start = ((), (), s32[]{:S(2)}) async-start(), calls=%async_computation.1 | async-start | bytes 9437184 | tf_op jit(solution)/shard_map/all_gather | solution.py:46
  7.9 361.5 %reduce-scatter.2.cloned.1.call-start = ((), (), s32[]{:S(2)}) async-start(), calls=%async_computation.2 | async-start | bytes 17301504 | tf_op jit(solution)/shard_map/reduce_scatter | solution.py:81
  11.9 3.7 copy-start.11
  14.2 1.3 copy-start.4
  16.8 25.1 %collective-permute-start = (f32[16,128,128]{2,1,0:T(8,128)S(1)}, f32[16,128,128]{2,1,0:T(8,128)}, u32[]{:S(2)}, u32[]{:S(2)}) collective-permute-start(f32[16,128,128]{2,1,0:T(8,128)S(1)} %fusion.25), channel_id=1, source_target_pairs={{0,8},{8,0},{16,24},{24,16},{1,9},{9,1},{17,25},{25,17},{2,10},{10... | collective-permute-start | bytes 3145736 | tf_op jit(solution)/shard_map/ppermute | solution.py:16
  20.1 30.4 %copy-start.20 = (f32[1,512,128]{1,2,0:T(8,128)}, f32[1,512,128]{1,2,0:T(8,128)S(1)}, u32[]{:S(2)}) copy-start(f32[1,512,128]{1,2,0:T(8,128)S(1)} %copy.80) | copy-start | bytes 786436
  44.5 47.9 %collective-permute-start.1 = (f32[16,128,128]{2,1,0:T(8,128)}, f32[16,128,128]{2,1,0:T(8,128)}, u32[]{:S(2)}, u32[]{:S(2)}) collective-permute-start(f32[16,128,128]{2,1,0:T(8,128)} %get-tuple-element.30), channel_id=1, source_target_pairs={{0,16},{8,24},{16,0},{24,8},{1,17},{9,25},{17,1},{25,9},{2,18},{10... | collective-permute-start | bytes 3145736 | tf_op jit(solution)/shard_map/ppermute | solution.py:16
  46.7 3.8 %copy-start.5 = (bf16[64,8,16,128]{3,2,1,0:T(8,128)(2,1)S(1)}, bf16[64,8,16,128]{3,2,1,0:T(8,128)(2,1)}, u32[]{:S(2)}) copy-start(bf16[64,8,16,128]{3,2,1,0:T(8,128)(2,1)} %copy-done.4) | copy-start | bytes 6291460
  49.1 9.6 %copy-start.7 = (bf16[64,8,16,128]{3,2,1,0:T(8,128)(2,1)}, bf16[64,8,16,128]{3,2,1,0:T(8,128)(2,1)S(1)}, u32[]{:S(2)}) copy-start(bf16[64,8,16,128]{3,2,1,0:T(8,128)(2,1)S(1)} %copy.126) | copy-start | bytes 6291460
  102.5 1.3 copy-start.2
  116.0 6.8 %copy-start.12 = (bf16[1,512,2048]{1,2,0:T(8,128)(2,1)S(1)}, bf16[1,512,2048]{1,2,0:T(8,128)(2,1)}, u32[]{:S(2)}) copy-start(bf16[1,512,2048]{1,2,0:T(8,128)(2,1)} %copy.123) | copy-start | bytes 6291460
  116.0 6.8 %copy-start.13 = (bf16[512,16,128]{0,2,1:T(8,128)(2,1)S(1)}, bf16[512,16,128]{0,2,1:T(8,128)(2,1)}, u32[]{:S(2)}) copy-start(bf16[512,16,128]{0,2,1:T(8,128)(2,1)} %copy.96) | copy-start | bytes 6291460
  140.9 3.2 copy-start.10
  152.3 1.6 copy-start.8
  154.4 1.6 copy-start.3
  156.0 7.0 %copy-start.16 = (f32[512,512]{0,1:T(8,128)S(1)}, f32[512,512]{0,1:T(8,128)}, u32[]{:S(2)}) copy-start(f32[512,512]{0,1:T(8,128)} %constant.30.clone) | copy-start | bytes 3145732
  156.0 7.0 %copy-start.17 = (f32[512,512]{0,1:T(8,128)S(1)}, f32[512,512]{0,1:T(8,128)}, u32[]{:S(2)}) copy-start(f32[512,512]{0,1:T(8,128)} %constant.7.clone) | copy-start | bytes 3145732
  156.0 7.0 %copy-start.18 = (f32[512,512]{0,1:T(8,128)S(1)}, f32[512,512]{0,1:T(8,128)}, u32[]{:S(2)}) copy-start(f32[512,512]{0,1:T(8,128)} %constant.8.clone) | copy-start | bytes 3145732
  156.0 7.0 %copy-start.19 = (f32[512,512]{0,1:T(8,128)S(1)}, f32[512,512]{0,1:T(8,128)}, u32[]{:S(2)}) copy-start(f32[512,512]{0,1:T(8,128)} %constant.9.clone) | copy-start | bytes 3145732
  161.8 69.3 %collective-permute-start.2 = (f32[2,16,128,128]{2,3,0,1:T(8,128)}, f32[2,16,128,128]{2,3,0,1:T(8,128)}, u32[]{:S(2)}, u32[]{:S(2)}) collective-permute-start(f32[2,16,128,128]{2,3,0,1:T(8,128)} %multiply_bitcast_fusion), channel_id=1, source_target_pairs={{0,8},{8,0},{16,24},{24,16},{1,9},{9,1},{17,25},{25,17},{2,10},{10... | collective-permute-start | bytes 6291464 | tf_op jit(solution)/shard_map/ppermute | solution.py:16
  163.0 9.4 %copy-start.21 = (f32[2,512,16]{1,0,2:T(2,128)S(1)}, f32[2,512,16]{1,0,2:T(2,128)}, u32[]{:S(2)}) copy-start(f32[2,512,16]{1,0,2:T(2,128)} %get-tuple-element.25) | copy-start | bytes 196612
  174.1 1.4 copy-start.15
  174.1 7.4 %slice-start = ((s8[8388608]{0:T(1024)(128)(4,1)}), s8[4194304]{0:T(1024)(128)(4,1)S(1)}, s32[]{:S(2)}) async-start(s8[8388608]{0:T(1024)(128)(4,1)} %bitcast.125), calls=%async_computation.3 | async-start | bytes 8388608
  175.5 6.1 %copy-start.6 = (bf16[64,8,16,128]{3,2,1,0:T(8,128)(2,1)S(1)}, bf16[64,8,16,128]{3,2,1,0:T(8,128)(2,1)}, u32[]{:S(2)}) copy-start(bf16[64,8,16,128]{3,2,1,0:T(8,128)(2,1)} %copy-done.4) | copy-start | bytes 6291460
  175.5 6.0 %slice-start.1 = ((s8[8388608]{0:T(1024)(128)(4,1)}), s8[4194304]{0:T(1024)(128)(4,1)S(1)}, s32[]{:S(2)}) async-start(s8[8388608]{0:T(1024)(128)(4,1)} %bitcast.125), calls=%async_computation.4 | async-start | bytes 8388608
  189.1 47.9 %copy-start.14 = (bf16[512,16,128]{0,2,1:T(8,128)(2,1)S(1)}, bf16[512,16,128]{0,2,1:T(8,128)(2,1)}, u32[]{:S(2)}) copy-start(bf16[512,16,128]{0,2,1:T(8,128)(2,1)} %copy.96) | copy-start | bytes 6291460
  231.1 14.1 %slice-start.2 = ((s8[8388608]{0:T(1024)(128)(4,1)}), s8[4194304]{0:T(1024)(128)(4,1)S(1)}, s32[]{:S(2)}) async-start(s8[8388608]{0:T(1024)(128)(4,1)} %bitcast.127), calls=%async_computation.5 | async-start | bytes 8388608
  233.9 11.3 %copy-start.9 = (bf16[64,8,16,128]{3,2,1,0:T(8,128)(2,1)S(1)}, bf16[64,8,16,128]{3,2,1,0:T(8,128)(2,1)}, u32[]{:S(2)}) copy-start(bf16[64,8,16,128]{3,2,1,0:T(8,128)(2,1)} %copy-done.7) | copy-start | bytes 6291460
  233.9 11.3 %slice-start.3 = ((s8[8388608]{0:T(1024)(128)(4,1)}), s8[4194304]{0:T(1024)(128)(4,1)S(1)}, s32[]{:S(2)}) async-start(s8[8388608]{0:T(1024)(128)(4,1)} %bitcast.127), calls=%async_computation.6 | async-start | bytes 8388608
  233.9 59.4 %collective-permute-start.3 = (f32[1,16,128,128]{2,3,0,1:T(8,128)}, f32[1,16,128,128]{2,3,0,1:T(8,128)}, u32[]{:S(2)}, u32[]{:S(2)}) collective-permute-start(f32[1,16,128,128]{2,3,0,1:T(8,128)} %slice_add_fusion), channel_id=1, source_target_pairs={{0,16},{8,24},{16,0},{24,8},{1,17},{9,25},{17,1},{25,9},{2,18},{10... | collective-permute-start | bytes 3145736 | tf_op jit(solution)/shard_map/ppermute | solution.py:16
  303.9 65.5 %copy-start.1 = (bf16[1,512,2048]{2,1,0:T(8,128)(2,1)S(1)}, bf16[1,512,2048]{2,1,0:T(8,128)(2,1)}, u32[]{:S(2)}) copy-start(bf16[1,512,2048]{2,1,0:T(8,128)(2,1)} %param.15) | copy-start | bytes 6291460
Sparse Core Ops, SparseCore 0:
  9.9 56.7 all-gather.1
  152.5 216.9 reduce-scatter.1
where the time goes:
time: 377 us; the launch traced here: 376 us
  waiting for transfers between devices  198 us (53%)
  matrix products  90.4 us (24%)
  local copies, waits for them, and re-layouts  43.6 us (12%)
  other arithmetic  21.1 us (6%)
  between operations  14.4 us (4%)
  starting transfers between devices  8.67 us (2%)
    ppermute x4, waiting for transfers between devices, swapped(): return lax.ppermute(value, axis, pairs)  141 us
    reduce_scatter x1, waiting for transfers between devices, local(): lax.psum_scatter(lax.dot_general(attn, grad_rows, (((0,), (0,)), ((), ())...  56.5 us
    unnamed x60, local copies, waits for them, and re-layouts  24.4 us
    dot_general x1, matrix products, local(): jnp.einsum('thd,shd->hts', grad_heads, value_heads, preferred_element_typ...  18.2 us
    reduce_sum x1, other arithmetic, local(): jnp.sum(energy * sel_mat[None], axis=2)  9.18 us
    ppermute x4, starting transfers between devices, swapped(): return lax.ppermute(value, axis, pairs)  8.59 us
    dot_general x1, matrix products, local(): jnp.einsum('hts,thd->shd', probs, grad_heads, preferred_element_type=jnp....  8.23 us
    dot_general x1, matrix products, local(): lax.dot_general(attn, grad_rows, (((0,), (0,)), ((), ())), preferred_elem...  8.18 us
  transfers between devices with their start and end apart: 6, of which 5 were waited for; matrix products, arithmetic and copies ran while one was open for 25% of the time, Pallas kernels for 0%

commit v1 on v0

v1 whole, which is shorter than its diff:
```python
import functools

import jax
import jax.numpy as jnp
from jax import lax
from jax.experimental import pallas as pl
from jax.experimental.pallas import tpu as pltpu
from jax.sharding import PartitionSpec as P

H = 16
HD = 128
GROUP = 64
LEVELS = 8
HALF = 2 * GROUP
TILE = 4 * GROUP
SCALE = HD ** (-0.5)
BF = jnp.bfloat16
F32 = jnp.float32


def swapped(value, axis, mask):
    return lax.ppermute(value, axis, [(source, source ^ mask) for source in range(lax.axis_size(axis))])


def mm(a, b, ca, cb):
    return lax.dot_general(a, b, (((ca,), (cb,)), ((), ())), preferred_element_type=F32)


def call(body, flops, nbytes, vmem=60, **kwargs):
    return pl.pallas_call(
        body,
        cost_estimate=pl.CostEstimate(flops=int(flops), bytes_accessed=int(nbytes), transcendentals=0),
        compiler_params=pltpu.CompilerParams(vmem_limit_bytes=vmem * 1024 * 1024),
        **kwargs,
    )


def level_columns(gain_ref, head, levels):
    rolled = pltpu.roll(gain_ref[...], lax.rem(LEVELS * H - head, LEVELS * H), 1)
    return {level: rolled[:, level * H : level * H + 1] for level in levels}


def half_masks():
    row = lax.broadcasted_iota(jnp.int32, (HALF, HALF), 0)
    col = lax.broadcasted_iota(jnp.int32, (HALF, HALF), 1)
    same = (row >= GROUP) == (col >= GROUP)
    return same & (col <= row), (row >= GROUP) & (col < GROUP)


def tile_weight(w, start, own, below):
    first, second = slice(start, start + HALF), slice(start + HALF, start + TILE)
    zero = jnp.zeros((HALF, HALF), F32)

    def corner(rows):
        return jnp.where(own, w[0][rows], jnp.where(below, w[1][rows], 0.0))

    side = jnp.broadcast_to(w[2][second], (HALF, HALF))
    top = jnp.concatenate([corner(first), zero], axis=1)
    bottom = jnp.concatenate([side, corner(second)], axis=1)
    return jnp.concatenate([top, bottom], axis=0)


def far_blocks(seg_len):
    blocks = []
    size, level = TILE, 3
    while size < seg_len:
        for start in range(0, seg_len, 2 * size):
            blocks.append((level, start + size, start, size))
        size, level = 2 * size, level + 1
    return blocks


def states_body(k_ref, v_ref, wide_ref, half_ref, block_ref):
    seg_len = k_ref.shape[0]
    for i in range(wide_ref.shape[0]):
        cols = slice(i * HD, (i + 1) * HD)
        tiles = [
            mm(k_ref[start : start + TILE, cols], v_ref[start : start + TILE, cols], 0, 0)
            for start in range(0, seg_len, TILE)
        ]
        state = sum(tiles[1:], tiles[0])
        wide_ref[i] = state
        half_ref[i] = state.astype(BF)
        for j, (_, _, col, size) in enumerate(far_blocks(seg_len)):
            part = tiles[col // TILE : (col + size) // TILE]
            block_ref[j, i] = sum(part[1:], part[0]).astype(BF)


def intra_body(n_bits, heads, bits_ref, q_ref, k_ref, v_ref, gain_ref, block_ref, out_ref, wq_ref):
    seg_len = q_ref.shape[0]
    loc_bits = (seg_len // GROUP).bit_length() - 1
    own, below = half_masks()
    for i in range(heads):
        cols = slice(i * HD, (i + 1) * HD)
        w = level_columns(gain_ref, pl.program_id(0) * heads + i, range(loc_bits + 1 + n_bits))
        for b in range(n_bits):
            factor = w[loc_bits + 1 + b] * bits_ref[b].astype(F32)
            at = (i * n_bits + b) * HD
            wq_ref[:, at : at + HD] = (q_ref[:, cols].astype(F32) * factor).astype(BF)
        for start in range(0, seg_len, TILE):
            rows = slice(start, start + TILE)
            scores = mm(q_ref[rows, cols], k_ref[rows, cols], 1, 1) * SCALE
            probs = (scores * tile_weight(w, start, own, below)).astype(BF)
            total = mm(probs, v_ref[rows, cols], 1, 0)
            for j, (level, row, _, size) in enumerate(far_blocks(seg_len)):
                if row <= start < row + size:
                    total += mm(q_ref[rows, cols], block_ref[j, i], 1, 0) * (w[level][rows] * SCALE)
            out_ref[rows, cols] = total


def attn_body(n_bits, heads, at_ref, wq_ref, intra_ref, *refs):
    far_refs, out_ref = refs[:n_bits], refs[n_bits]
    for i in range(heads):
        cols = slice(i * HD, (i + 1) * HD)
        far = jnp.concatenate([ref[i] for ref in far_refs], axis=0)
        total = intra_ref[:, cols] + mm(wq_ref[:, i * n_bits * HD : (i + 1) * n_bits * HD], far, 1, 0) * SCALE
        place = pl.multiple_of((i ^ at_ref[1]) * HD, HD)
        out_ref[:, pl.ds(place, HD)] = total.astype(BF)


def weight_body(picks, core_ref, attn_ref, attn2_ref, gx_ref, gx2_ref, gy_ref, gy2_ref, outx_ref, outy_ref):
    del core_ref
    for pick, left, right, out_ref in (
        (picks[0], gx_ref, gx2_ref, outx_ref),
        (picks[1], gy_ref, gy2_ref, outy_ref),
    ):
        total = 0.0
        for ref, grad_ref in ((attn_ref, left), (attn2_ref, right)):
            lhs = jnp.concatenate([ref[:, p * HD : (p + 1) * HD] for p in pick], axis=1)
            total += mm(lhs, grad_ref[...], 0, 0)
        out_ref[...] = total.astype(out_ref.dtype)


def attn_grad_body(count, at_ref, dout_ref, *refs):
    del at_ref
    out_ref = refs[-1]
    for j in range(count):
        @pl.when(pl.program_id(0) == j)
        def _(j=j):
            out_ref[...] = mm(dout_ref[...], refs[j][...], 1, 1).astype(BF)


def far_grad_body(n_bits, heads, wq_ref, g_ref, half_ref, wide_ref):
    for i in range(heads):
        span = n_bits * HD
        grad = mm(wq_ref[:, i * span : (i + 1) * span], g_ref[:, i * HD : (i + 1) * HD], 0, 0) * SCALE
        for b in range(n_bits):
            part = grad[b * HD : (b + 1) * HD]
            half_ref[b, i] = part.astype(BF)
            wide_ref[b, i] = part


def far_grad_four_body(heads, at_ref, wq_ref, g_ref, half_ref, wide_ref):
    for i in range(heads):
        grad = mm(wq_ref[:, 2 * i * HD : 2 * (i + 1) * HD], g_ref[:, i * HD : (i + 1) * HD], 0, 0) * SCALE
        low, high = grad[:HD], grad[HD:]
        half_ref[i] = jnp.where(at_ref[0] == 2, high, low).astype(BF)
        wide_ref[i] = high


def main_body(n_bits, heads, offset, carried, bits_ref, q_ref, k_ref, v_ref, g_ref, gain_ref, block_ref, *refs):
    far_refs = refs[:n_bits]
    gq_ref, gk_ref, gv_ref, back_ref, gain_grad_ref, lev_ref = refs[n_bits + carried :]
    seg_len = q_ref.shape[0]
    loc_bits = (seg_len // GROUP).bit_length() - 1
    own, below = half_masks()
    lane = lax.broadcasted_iota(jnp.int32, (1, LEVELS * H), 1)

    @pl.when(pl.program_id(0) == 0)
    def _():
        if carried:
            gain_grad_ref[...] = refs[n_bits + carried - 1][...]
        else:
            gain_grad_ref[...] = jnp.zeros_like(gain_grad_ref)

    lev_ref[...] = jnp.zeros_like(lev_ref)

    def row_sum(x):
        return jnp.sum(x, axis=1, keepdims=True)

    for i in range(heads):
        head = offset + pl.program_id(0) * heads + i
        cols = slice(i * HD, (i + 1) * HD)
        w = level_columns(gain_ref, head, range(loc_bits + 1 + n_bits))
        far = jnp.concatenate([ref[i] for ref in far_refs], axis=0)

        def put(rows, column, level, head=head):
            pick = (lane == level * H + head).astype(F32)
            lev_ref[rows] += column * pick

        for start in range(0, seg_len, TILE):
            rows = slice(start, start + TILE)
            first, second = slice(start, start + HALF), slice(start + HALF, start + TILE)
            q, g = q_ref[rows, cols], g_ref[rows, cols]
            q_wide = q.astype(F32)
            back = mm(g, far, 1, 1)
            total = jnp.zeros((TILE, HD), F32)
            for b in range(n_bits):
                term = back[:, b * HD : (b + 1) * HD]
                bit = bits_ref[b].astype(F32)
                put(rows, row_sum(q_wide * term) * (SCALE * bit), loc_bits + 1 + b)
                total += term * (w[loc_bits + 1 + b][rows] * bit)
            for j, (level, row, _, size) in enumerate(far_blocks(seg_len)):
                if row <= start < row + size:
                    term = mm(g, block_ref[j, i], 1, 1)
                    put(rows, row_sum(q_wide * term) * SCALE, level)
                    total += term * w[level][rows]
            weight = tile_weight(w, start, own, below)
            scores = mm(q, k_ref[rows, cols], 1, 1) * SCALE
            prob_grad = mm(g, v_ref[rows, cols], 1, 1)
            energy = scores * prob_grad
            for half, at in ((first, 0), (second, HALF)):
                corner = energy[at : at + HALF, at : at + HALF]
                put(half, row_sum(jnp.where(own, corner, 0.0)), 0)
                put(half, row_sum(jnp.where(below, corner, 0.0)), 1)
            put(second, row_sum(energy[HALF:, :HALF]), 2)
            probs = (scores * weight).astype(BF)
            score_grad = (prob_grad * weight).astype(BF)
            total += mm(score_grad, k_ref[rows, cols], 1, 0)
            gq_ref[rows, cols] = (total * SCALE).astype(BF)
            gk_ref[rows, cols] = mm(score_grad, q, 0, 0) * SCALE
            gv_ref[rows, cols] = mm(probs, g, 0, 0)
        for j, (level, row, _, size) in enumerate(far_blocks(seg_len)):
            rows = slice(row, row + size)
            weighted = (q_ref[rows, cols].astype(F32) * w[level][rows]).astype(BF)
            back_ref[j, i] = mm(weighted, g_ref[rows, cols], 0, 0) * SCALE
    gain_grad_ref[...] += lev_ref[...]


def final_body(heads, shares_ref, k_ref, v_ref, gk_ref, gv_ref, back_ref, *refs):
    got_refs, (key_ref, value_ref) = refs[:-2], refs[-2:]
    seg_len = k_ref.shape[0]
    for i in range(heads):
        cols = slice(i * HD, (i + 1) * HD)
        state = jnp.zeros((HD, HD), F32)
        for b, ref in enumerate(got_refs):
            state += ref[i].astype(F32) * shares_ref[b].astype(F32)
        for start in range(0, seg_len, TILE):
            rows = slice(start, start + TILE)
            here = state
            for j, (_, _, col, size) in enumerate(far_blocks(seg_len)):
                if col <= start < col + size:
                    here = here + back_ref[j, i]
            half = here.astype(BF)
            key_ref[rows, cols] = (gk_ref[rows, cols] + mm(v_ref[rows, cols], half, 1, 1)).astype(BF)
            value_ref[rows, cols] = (gv_ref[rows, cols] + mm(k_ref[rows, cols], half, 1, 0)).astype(BF)


def sds(shape, dtype):
    return jax.ShapeDtypeStruct(shape, dtype)


def local(queries, keys, values, level_gain, out_weight, out_grad):
    outs = step(queries[0], keys[0], values[0], level_gain[0], out_weight, out_grad[0])
    return tuple(x[None] for x in outs[:4]) + (outs[4],)


def is_fast(seq_count, batch_count):
    return batch_count == 8 and seq_count * batch_count == 2 * H


def step(q, k, v, gain, out_weight, dout):
    seg_len, width = q.shape
    seq_count, batch_count = lax.axis_size("seq"), lax.axis_size("batch")
    n_bits = seq_count.bit_length() - 1
    seg_index, batch_index = lax.axis_index("seq"), lax.axis_index("batch")
    bits = jnp.stack([seg_index >> b & 1 for b in range(n_bits)]).astype(jnp.int32)
    fast = is_fast(seq_count, batch_count)
    prefetch = pltpu.PrefetchScalarGridSpec
    tok_bytes = seg_len * width * 2
    head_flops = 2 * seg_len * HD * HD * H
    n_blocks = len(far_blocks(seg_len))
    mats = (H, HD, HD)

    def cols(heads, scale=1):
        return pl.BlockSpec((seg_len, heads * HD * scale), lambda h, *_: (0, h))

    def mat(heads):
        return pl.BlockSpec((heads, HD, HD), lambda h, *_: (h, 0, 0))

    def stack(count, heads):
        return pl.BlockSpec((count, heads, HD, HD), lambda h, *_: (0, h, 0, 0))

    whole_gain = pl.BlockSpec((seg_len, LEVELS * H), lambda h, *_: (0, 0))

    state_wide, state_half, blocks = call(
        states_body, head_flops, 2 * tok_bytes,
        out_shape=(sds(mats, F32), sds(mats, BF), sds((n_blocks,) + mats, BF)),
        grid=(H // 4,), in_specs=[cols(4), cols(4)],
        out_specs=(mat(4), mat(4), stack(n_blocks, 4)),
    )(k, v)
    fars = []
    running_wide, running = state_wide, state_half
    for b in range(n_bits):
        received = swapped(running, "seq", 1 << b)
        fars.append(received)
        if b + 1 < n_bits:
            running_wide = running_wide + received.astype(F32)
            running = running_wide.astype(BF)

    if fast:
        pieces = {0: out_weight}
        rows = out_weight.shape[0]
        dout_pair = swapped(dout, "batch", 1)
        pieces[2] = swapped(out_weight, "batch", 2)
        pieces[4] = swapped(out_weight, "batch", 4)
        pieces[1] = swapped(out_weight, "batch", 1)
        diag_low = swapped(pieces[2][: rows // 2], "batch", 4)
        diag_high = swapped(pieces[4][rows // 2 :], "batch", 2)
        pieces[3] = swapped(pieces[2], "batch", 1)
        pieces[5] = swapped(pieces[4], "batch", 1)
        diag_low_pair = swapped(diag_low, "batch", 1)
        diag_high_pair = swapped(diag_high, "batch", 1)
        stages = [
            [(pieces[m], batch_index ^ m) for m in (0, 1)],
            [(pieces[m], batch_index ^ m) for m in (2, 3, 4, 5)],
            [
                (diag_low, (batch_index ^ 6) * 2),
                (diag_high, (batch_index ^ 6) * 2 + 1),
                (diag_low_pair, (batch_index ^ 7) * 2),
                (diag_high_pair, (batch_index ^ 7) * 2 + 1),
            ],
        ]
        g = None
        for stage in stages:
            count, piece_rows = len(stage), stage[0][0].shape[0]
            index = jnp.stack([at for _, at in stage]).astype(jnp.int32)
            arrays = [array for array, _ in stage]
            extra = [] if g is None else [g]
            g = call(
                functools.partial(attn_grad_body, count),
                2 * seg_len * width * piece_rows * count, tok_bytes + count * piece_rows * (width + seg_len) * 2,
                out_shape=sds((seg_len, width), BF),
                grid_spec=prefetch(
                    num_scalar_prefetch=1, grid=(count,),
                    in_specs=[pl.BlockSpec((seg_len, width), lambda j, at: (0, 0))]
                    + [pl.BlockSpec((piece_rows, width), lambda j, at: (0, 0))] * count
                    + [pl.BlockSpec(memory_space=pl.ANY)] * len(extra),
                    out_specs=pl.BlockSpec((seg_len, piece_rows), lambda j, at: (0, at[j])),
                ),
                input_output_aliases={} if g is None else {2 + count: 0},
            )(index, dout, *arrays, *extra)
    else:
        gathered = lax.all_gather(out_weight, "batch", axis=0, tiled=True)
        g = mm(dout, gathered, 1, 1).astype(BF)

    intra, wq = call(
        functools.partial(intra_body, n_bits, 4), 4 * seg_len * TILE * width, 7 * tok_bytes,
        out_shape=(sds((seg_len, width), F32), sds((seg_len, n_bits * width), BF)),
        grid_spec=prefetch(
            num_scalar_prefetch=1, grid=(H // 4,),
            in_specs=[cols(4), cols(4), cols(4), whole_gain, stack(n_blocks, 4)],
            out_specs=(cols(4), cols(4, n_bits)),
        ),
    )(bits, q, k, v, gain, blocks)

    at = jnp.stack([seg_index, batch_index >> 1]).astype(jnp.int32)
    if not fast:
        at = jnp.zeros_like(at)
    attn = call(
        functools.partial(attn_body, n_bits, 4), head_flops * n_bits, 5 * tok_bytes,
        out_shape=sds((seg_len, width), BF),
        grid_spec=prefetch(
            num_scalar_prefetch=1, grid=(H // 4,),
            in_specs=[
                pl.BlockSpec((seg_len, 4 * HD * n_bits), lambda j, a: (0, j ^ a[0])),
                pl.BlockSpec((seg_len, 4 * HD), lambda j, a: (0, j ^ a[0])),
            ]
            + [pl.BlockSpec((4, HD, HD), lambda j, a: (j ^ a[0], 0, 0))] * n_bits,
            out_specs=pl.BlockSpec((seg_len, 4 * HD), lambda j, a: (0, j)),
        ),
    )(at, wq, intra, *fars)

    if fast:
        weight_grad = reduce_weight(attn, dout, dout_pair, batch_index, seq_count)
    else:
        weight_grad = lax.psum_scatter(
            mm(attn, dout, 0, 0), ("seq", "batch"), scatter_dimension=0, tiled=True
        )

    if fast:
        far_half, far_wide = call(
            functools.partial(far_grad_four_body, 4), head_flops * n_bits, 4 * tok_bytes,
            out_shape=(sds(mats, BF), sds(mats, F32)),
            grid_spec=prefetch(
                num_scalar_prefetch=1, grid=(H // 4,),
                in_specs=[cols(4, n_bits), cols(4)], out_specs=(mat(4), mat(4)),
            ),
        )(seg_index.astype(jnp.int32)[None], wq, g)
        near = lax.ppermute(far_half, "seq", [(1, 0), (3, 2), (2, 3)])
        both = (far_wide + near.astype(F32)).astype(BF)
        got = [near, lax.ppermute(both, "seq", [(3, 1)]), lax.ppermute(both, "seq", [(3, 0)])]
        shares = jnp.stack([1 - bits[0], jnp.int32(1), jnp.int32(1)])
    else:
        far_half, far_wide = call(
            functools.partial(far_grad_body, n_bits, 4), head_flops * n_bits, 4 * tok_bytes,
            out_shape=(sds((n_bits,) + mats, BF), sds((n_bits,) + mats, F32)),
            grid=(H // 4,), in_specs=[cols(4, n_bits), cols(4)],
            out_specs=(stack(n_bits, 4),) * 2,
        )(wq, g)
        got = []
        pending_half, pending_wide = far_half, far_wide
        for b in range(n_bits):
            received = swapped(pending_half, "seq", 1 << b)
            got.append(received[0])
            if b + 1 < n_bits:
                pending_wide = pending_wide[1:] + received[1:].astype(F32)
                pending_half = pending_wide.astype(BF)
        shares = 1 - bits

    done = []
    for part in range(2):
        first = part * (H // 4)
        two = pl.BlockSpec((seg_len, 2 * HD), lambda h, *_, first=first: (0, h + first))
        two_mats = pl.BlockSpec((2, HD, HD), lambda h, *_, first=first: (h + first, 0, 0))
        two_blocks = pl.BlockSpec((n_blocks, 2, HD, HD), lambda h, *_, first=first: (0, h + first, 0, 0))
        done = call(
            functools.partial(main_body, n_bits, 2, first * 2, len(done)),
            5 * seg_len * TILE * width + head_flops * 2, 5 * tok_bytes,
            out_shape=(
                sds((seg_len, width), BF), sds((seg_len, width), F32), sds((seg_len, width), F32),
                sds((n_blocks,) + mats, F32), sds((seg_len, LEVELS * H), F32),
            ),
            grid_spec=prefetch(
                num_scalar_prefetch=1, grid=(H // 4,),
                in_specs=[two] * 4 + [whole_gain, two_blocks] + [two_mats] * n_bits
                + ([pl.BlockSpec(memory_space=pl.ANY)] * 4 + [whole_gain] if done else []),
                out_specs=(two, two, two, two_blocks, whole_gain),
                scratch_shapes=[pltpu.VMEM((seg_len, LEVELS * H), F32)],
            ),
            input_output_aliases={7 + n_bits + i: i for i in range(4)} if done else {},
        )(bits, q, k, v, g, gain, blocks, *fars, *done)
    query_grad, key_in, value_in, back, gain_grad = done

    key_grad, value_grad = call(
        functools.partial(final_body, 4), 2 * head_flops, 8 * tok_bytes,
        out_shape=(sds((seg_len, width), BF),) * 2,
        grid_spec=prefetch(
            num_scalar_prefetch=1, grid=(H // 4,),
            in_specs=[cols(4)] * 4 + [stack(n_blocks, 4)] + [mat(4)] * len(got),
            out_specs=(cols(4), cols(4)),
        ),
    )(shares, k, v, key_in, value_in, back, *got)
    return query_grad, key_grad, value_grad, gain_grad, weight_grad


def reduce_weight(attn, dout, dout_pair, batch_index, seq_count):
    seg_len, width = attn.shape
    quarter = width // 4
    core = batch_index & 1
    attn_pair = swapped(attn, "batch", 1)
    half = core.astype(jnp.int32)[None]

    def products(picks, dtype):
        lhs = pl.BlockSpec((seg_len, 4 * HD), lambda j, c: (0, j))
        grads = [pl.BlockSpec((seg_len, quarter), lambda j, c, n=n: (0, 2 * c[0] + n)) for n in (0, 0, 1, 1)]
        out = pl.BlockSpec((2 * HD, quarter), lambda j, c: (j, 0))
        return call(
            functools.partial(weight_body, picks), 4 * seg_len * width * quarter,
            2 * seg_len * (width + 2 * quarter) * 2 + width * quarter * 2,
            out_shape=(sds((width // 2, quarter), dtype),) * 2,
            grid_spec=pltpu.PrefetchScalarGridSpec(
                num_scalar_prefetch=1, grid=(width // (4 * HD),),
                in_specs=[lhs, lhs] + grads, out_specs=(out, out),
            ),
        )(half, attn, attn_pair, dout, dout_pair, dout, dout_pair)

    send_x, send_y = products(((1, 3), (2, 3)), BF)
    got_x = swapped(send_x, "batch", 2)
    got_y = swapped(send_y, "batch", 4)
    keep_x, keep_y = products(((0, 2), (0, 1)), F32)

    def pick(array, which):
        return array.reshape(seq_count, 2, HD, quarter)[:, which].astype(F32)

    send_xy = (pick(keep_x, 1) + pick(got_x, 1)).astype(BF)
    send_yx = (pick(keep_y, 1) + pick(got_y, 1)).astype(BF)
    got_xy = swapped(send_xy, "batch", 4)
    got_yx = swapped(send_yx, "batch", 2)
    left = pick(keep_x, 0) + pick(got_x, 0) + got_xy.astype(F32)
    right = pick(keep_y, 0) + pick(got_y, 0) + got_yx.astype(F32)
    total = jnp.concatenate([left, right], axis=2).reshape(2, 2, HD, width // 2)
    got_z = swapped(total[:, 1].astype(BF), "seq", 1).astype(F32)
    got_zz = swapped((total[1, 0] + got_z[1]).astype(BF), "seq", 2).astype(F32)
    mine = total[0, 0] + got_z[0] + got_zz
    rows = mine.shape[0] // 2
    other = swapped(lax.dynamic_slice_in_dim(mine, (1 - core) * rows, rows, 0), "batch", 1)
    own = lax.dynamic_slice_in_dim(mine, core * rows, rows, 0)
    return jnp.where(
        core == 0, jnp.concatenate([own, other], axis=1), jnp.concatenate([other, own], axis=1)
    )


def solution(mesh):
    row = P("batch", "seq", None)
    return jax.shard_map(
        local,
        mesh=mesh,
        in_specs=(row, row, row, row, P("batch", None), row),
        out_specs=(row, row, row, row, P(("seq", "batch"), None)),
        check_vma=False,
    )
```

time: 377 us -> 219 us (0.58)
  waiting for transfers between devices: 198 us -> 62.7 us
  Pallas kernels: 0 us -> 99.9 us
  matrix products: 90.4 us -> 0 us
  local copies, waits for them, and re-layouts: 43.6 us -> 6.69 us
  starting transfers between devices: 8.67 us -> 30.7 us
  between operations: 14.4 us -> 0.82 us
  other arithmetic: 21.1 us -> 16.3 us
    pallas_call x0 -> x12, Pallas kernels: none -> 99.9 us  [the longest x2 30.1 us: step(): call(functools.partial(main_body, n_bits, 2, first * 2, len(done)), 5 * s...]
    dot_general x14 -> x0, matrix products: 90.4 us -> none  [the longest x1 18.2 us: local(): jnp.einsum('thd,shd->hts', grad_heads, value_heads, preferred_element_typ...]
    ppermute x4 -> x23, waiting for transfers between devices: 141 us -> 62.7 us  [the longest x20 48.7 us: swapped(): lax.ppermute(value, axis, [(source, source ^ mask) for source in range(la...]
    reduce_scatter x1 -> x0, waiting for transfers between devices: 56.5 us -> none  [local(): lax.psum_scatter(lax.dot_general(attn, grad_rows, (((0,), (0,)), ((), ())...]
    ppermute x4 -> x23, starting transfers between devices: 8.59 us -> 30.7 us  [the longest x20 27.4 us: swapped(): lax.ppermute(value, axis, [(source, source ^ mask) for source in range(la...]
    unnamed x60 -> x18, local copies, waits for them, and re-layouts: 24.4 us -> 2.41 us
    reduce_sum x1 -> x0, other arithmetic: 9.18 us -> none  [local(): jnp.sum(energy * sel_mat[None], axis=2)]
    convert_element_type x3 -> x6, other arithmetic: 2.66 us -> 8.96 us  [the longest x1 2.37 us: reduce_weight(): send_yx = (pick(keep_y, 1) + pick(got_y, 1)).astype(BF)]
  transfers between devices with their start and end apart: 6 -> 23, of which waited for: 5 -> 8; matrix products, arithmetic and copies ran while one was open for 25% -> 8% of each run, Pallas kernels for 0% -> 44%
where the time goes in v1:
time: 219 us; the launch traced here: 217 us
  Pallas kernels  99.9 us (46%)
  waiting for transfers between devices  62.7 us (29%)
  starting transfers between devices  30.7 us (14%)
  other arithmetic  16.3 us (7%)
  local copies, waits for them, and re-layouts  6.69 us (3%)
    ppermute x20, waiting for transfers between devices, swapped(): lax.ppermute(value, axis, [(source, source ^ mask) for source in range(la...  48.7 us
    pallas_call x2, Pallas kernels, step(): call(functools.partial(main_body, n_bits, 2, first * 2, len(done)), 5 * s...  30.1 us
    ppermute x20, starting transfers between devices, swapped(): lax.ppermute(value, axis, [(source, source ^ mask) for source in range(la...  27.4 us
    pallas_call x3, Pallas kernels, step(): call(functools.partial(attn_grad_body, count), 2 * seg_len * width * piec...  19 us
    ppermute x1, waiting for transfers between devices, step(): near = lax.ppermute(far_half, 'seq', [(1, 0), (3, 2), (2, 3)])  14 us
    pallas_call x2, Pallas kernels, products(): call(functools.partial(weight_body, picks), 4 * seg_len * width * quarter...  12.6 us
    pallas_call x1, Pallas kernels, step(): call(functools.partial(intra_body, n_bits, 4), 4 * seg_len * TILE * width...  12.6 us
    pallas_call x1, Pallas kernels, step(): call(functools.partial(final_body, 4), 2 * head_flops, 8 * tok_bytes, out...  8.62 us
  transfers between devices with their start and end apart: 23, of which 8 were waited for; matrix products, arithmetic and copies ran while one was open for 8% of the time, Pallas kernels for 44%

profile of v1, /device:TPU:1, one launch (start us, length us, event | category | flops | bytes accessed | tf_op | source)
XLA Modules:
  0.0 217.2 jit_solution(3621537069586679180)
XLA Ops:
  0.6 4.8 %shard_map.104 = (f32[16,128,128]{2,1,0:T(8,128)}, bf16[16,128,128]{2,1,0:T(8,128)(2,1)}, bf16[1,16,128,128]{3,2,1,0:T(8,128)(2,1)}) custom-call(bf16[512,2048]{1,0:T(8,128)(2,1)} %bitcast.108, bf16[512,2048]{1,0:T(8,128)(2,1)} %bitcast.113), custom_call_target="tpu_custom_call" | custom-call | flops 268435456 | bytes 4194304 | tf_op jit(solution)/shard_map/pallas_call | solution.py:286
  5.4 2.1 collective-permute-start.9
  7.6 11.8 %collective-permute-done.9.refs_0_ = bf16[16,128,128]{2,1,0:T(8,128)(2,1)S(1)} collective-permute-done((bf16[16,128,128]{2,1,0:T(8,128)(2,1)}, bf16[16,128,128]{2,1,0:T(8,128)(2,1)S(1)}, u32[]{:S(2)}, u32[]{:S(2)}) %collective-permute-start.9) | collective-permute-done | bytes 524320 | tf_op jit(solution)/shard_map/ppermute | solution.py:22
  19.4 2.3 %add_convert_fusion.1 = bf16[16,128,128]{2,1,0:T(8,128)(2,1)} fusion(f32[16,128,128]{2,1,0:T(8,128)} %get-tuple-element.30, bf16[16,128,128]{2,1,0:T(8,128)(2,1)S(1)} %collective-permute-done.9.refs_0_), kind=kLoop, calls=%fused_computation.16 | loop fusion | flops 786432 | bytes 2097152 | tf_op jit(solution)/shard_map/convert_element_type | solution.py:299
  21.7 2.2 %collective-permute-start.10 = (bf16[16,128,128]{2,1,0:T(8,128)(2,1)}, bf16[16,128,128]{2,1,0:T(8,128)(2,1)S(1)}, u32[]{:S(2)}, u32[]{:S(2)}) collective-permute-start(bf16[16,128,128]{2,1,0:T(8,128)(2,1)} %add_convert_fusion.1), channel_id=1, source_target_pairs={{0,16},{8,24},{16,0},{24,8},{1,17},{9,25},{17,1},{25,9},{2,18},{10... | collective-permute-start | bytes 1572872 | tf_op jit(solution)/shard_map/ppermute | solution.py:22
  23.9 1.8 collective-permute-start.15
  26.4 12.6 %shard_map.107 = (f32[512,2048]{1,0:T(8,128)}, bf16[512,4096]{1,0:T(8,128)(2,1)}) custom-call(s32[2]{0:T(128)} %pad_add_fusion.bits_ref, bf16[512,2048]{1,0:T(8,128)(2,1)} %bitcast.118, bf16[512,2048]{1,0:T(8,128)(2,1)} %bitcast.109, bf16[512,2048]{1,0:T(8,128)(2,1)} %bitcast.114, f32[512,128]{1,0:T(8,128)} %bitcast.124, ...), custom_call_target="tpu_custom_call" | custom-call | flops 1073741824 | bytes 14680064 | tf_op jit(solution)/shard_map/pallas_call | solution.py:347
  39.6 7.5 %collective-permute-done.10.refs_1_ = bf16[16,128,128]{2,1,0:T(8,128)(2,1)S(1)} collective-permute-done((bf16[16,128,128]{2,1,0:T(8,128)(2,1)}, bf16[16,128,128]{2,1,0:T(8,128)(2,1)S(1)}, u32[]{:S(2)}, u32[]{:S(2)}) %collective-permute-start.10) | collective-permute-done | bytes 524320 | tf_op jit(solution)/shard_map/ppermute | solution.py:22
  47.8 6.8 %shard_map.110.attn_ref = bf16[512,2048]{1,0:T(8,128)(2,1)} custom-call(s32[2]{0:T(128)} %pad_add_fusion.4.at_ref, bf16[512,4096]{1,0:T(8,128)(2,1)} %get-tuple-element.40.wq_ref, f32[512,2048]{1,0:T(8,128)} %get-tuple-element.46.intra_ref, bf16[16,128,128]{2,1,0:T(8,128)(2,1)} %copy-done.1, bf16[16,128,128]{2,1,0:T(8,128)(2,1)} %copy-done.2), custom_call_target="tpu_custom_call" | custom-call | flops 536870912 | bytes 10485760 | tf_op jit(solution)/shard_map/pallas_call | solution.py:360
  58.3 1.8 collective-permute-done.14.attn2_ref
  60.1 6.2 %shard_map.112 = (bf16[1024,512]{1,0:T(8,128)(2,1)}, bf16[1024,512]{1,0:T(8,128)(2,1)}) custom-call(s32[1]{0:T(128)} %bitcast.23.core_ref, bf16[512,2048]{1,0:T(8,128)(2,1)} %shard_map.110.attn_ref, bf16[512,2048]{1,0:T(8,128)(2,1)} %collective-permute-done.14.attn2_ref, bf16[512,2048]{1,0:T(8,128)(2,1)} %bitcast.100, ...), custom_call_target="tpu_custom_call" | custom-call | flops 2147483648 | bytes 8388608 | tf_op jit(solution)/shard_map/pallas_call | solution.py:458
  70.2 10.8 %collective-permute-done.refs_0_ = bf16[256,2048]{1,0:T(8,128)(2,1)S(1)} collective-permute-done((bf16[256,2048]{1,0:T(8,128)(2,1)}, bf16[256,2048]{1,0:T(8,128)(2,1)S(1)}, u32[]{:S(2)}, u32[]{:S(2)}) %collective-permute-start) | collective-permute-done | bytes 1048608 | tf_op jit(solution)/shard_map/ppermute | solution.py:22
  83.1 1.9 slice.62
  86.2 6.4 %shard_map.111 = (f32[1024,512]{1,0:T(8,128)}, f32[1024,512]{1,0:T(8,128)}) custom-call(s32[1]{0:T(128)} %bitcast.23.core_ref, bf16[512,2048]{1,0:T(8,128)(2,1)} %shard_map.110.attn_ref, bf16[512,2048]{1,0:T(8,128)(2,1)} %collective-permute-done.14.attn2_ref, bf16[512,2048]{1,0:T(8,128)(2,1)} %bitcast.102, ...), custom_call_target="tpu_custom_call" | custom-call | flops 2147483648 | bytes 8388608 | tf_op jit(solution)/shard_map/pallas_call | solution.py:458
  92.6 11.8 %collective-permute-done.18 = bf16[1024,512]{1,0:T(8,128)(2,1)} collective-permute-done((bf16[1024,512]{1,0:T(8,128)(2,1)}, bf16[1024,512]{1,0:T(8,128)(2,1)}, u32[]{:S(2)}, u32[]{:S(2)}) %collective-permute-start.18) | collective-permute-done | bytes 1048608 | tf_op jit(solution)/shard_map/ppermute | solution.py:22
  104.3 2.4 %fusion.10 = bf16[4,128,512]{2,1,0:T(8,128)(2,1)} fusion(f32[4,2,128,512]{3,2,1,0:T(8,128)} %bitcast.130, bf16[4,2,128,512]{3,2,1,0:T(8,128)(2,1)} %bitcast.30), kind=kLoop, calls=%fused_computation.18 | loop fusion | flops 786432 | bytes 2097152 | tf_op jit(solution)/shard_map/convert_element_type | solution.py:477
  107.1 2.0 fusion.9
  111.5 2.4 %collective-permute-start.6 = (bf16[256,2048]{1,0:T(8,128)(2,1)S(1)}, bf16[256,2048]{1,0:T(8,128)(2,1)}, u32[]{:S(2)}, u32[]{:S(2)}) collective-permute-start(bf16[256,2048]{1,0:T(8,128)(2,1)S(1)} %collective-permute-done.refs_0_), channel_id=1, source_target_pairs={{0,1},{1,0},{2,3},{3,2},{4,5},{5,4},{6,7},{7,6},{8,9},{9,8},{10,11... | collective-permute-start | bytes 3145736 | tf_op jit(solution)/shard_map/ppermute | solution.py:22
  113.9 1.6 collective-permute-done.1.refs_0_
  115.6 1.9 collective-permute-start.7
  117.4 5.1 %shard_map.101.refs_4_ = bf16[512,2048]{1,0:T(8,128)(2,1)} custom-call(s32[2]{0:T(128)} %pad_add_fusion.3.at_ref, bf16[512,2048]{1,0:T(8,128)(2,1)} %bitcast.104, bf16[256,2048]{1,0:T(8,128)(2,1)} %refs_0_.1, bf16[256,2048]{1,0:T(8,128)(2,1)} %collective-permute-done.8.refs_1_), custom_call_target="tpu_custom_call" | custom-call | flops 1073741824 | bytes 4718592 | tf_op jit(solution)/shard_map/pallas_call | solution.py:330
  122.5 3.4 %collective-permute-done.19 = bf16[4,128,512]{2,1,0:T(8,128)(2,1)} collective-permute-done((bf16[4,128,512]{2,1,0:T(8,128)(2,1)}, bf16[4,128,512]{2,1,0:T(8,128)(2,1)}, u32[]{:S(2)}, u32[]{:S(2)}) %collective-permute-start.19) | collective-permute-done | bytes 524320 | tf_op jit(solution)/shard_map/ppermute | solution.py:22
  126.8 1.7 fusion.3
  128.6 1.4 fusion.8
  131.4 7.3 %shard_map.102.refs_4_ = bf16[512,2048]{1,0:T(8,128)(2,1)} custom-call(s32[4]{0:T(128)} %pad_add_fusion.2.at_ref, bf16[512,2048]{1,0:T(8,128)(2,1)} %bitcast.105, bf16[256,2048]{1,0:T(8,128)(2,1)} %copy-done.3, bf16[256,2048]{1,0:T(8,128)(2,1)} %collective-permute-done.6.refs_1_, ...), custom_call_target="tpu_custom_call", output_to_operand_aliasing={{}: (6, {})} | custom-call | flops 2147483648 | bytes 7340032 | tf_op jit(solution)/shard_map/pallas_call | solution.py:330
  139.5 6.6 %shard_map.103.g_ref = bf16[512,2048]{1,0:T(8,128)(2,1)} custom-call(s32[4]{0:T(128)} %pad_add_fusion.1.at_ref, bf16[512,2048]{1,0:T(8,128)(2,1)} %bitcast.106, bf16[128,2048]{1,0:T(8,128)(2,1)} %collective-permute-done.1.refs_0_, bf16[128,2048]{1,0:T(8,128)(2,1)} %collective-permute-done.3.refs_1_, ...), custom_call_target="tpu_custom_call", output_to_operand_aliasing={{}: (6, {})} | custom-call | flops 1073741824 | bytes 4718592 | tf_op jit(solution)/shard_map/pallas_call | solution.py:330
  146.1 5.4 %shard_map.108 = (bf16[16,128,128]{2,1,0:T(8,128)(2,1)}, f32[16,128,128]{2,1,0:T(8,128)}) custom-call(s32[1]{0:T(128)} %bitcast.19.at_ref, bf16[512,4096]{1,0:T(8,128)(2,1)} %get-tuple-element.40.wq_ref, bf16[512,2048]{1,0:T(8,128)(2,1)} %shard_map.103.g_ref), custom_call_target="tpu_custom_call" | custom-call | flops 536870912 | bytes 8388608 | tf_op jit(solution)/shard_map/pallas_call | solution.py:382
  154.7 3.7 %collective-permute-start.21 = (bf16[128,1024]{1,0:T(8,128)(2,1)S(1)}, bf16[128,1024]{1,0:T(8,128)(2,1)S(1)}, u32[]{:S(2)}, u32[]{:S(2)}) collective-permute-start(bf16[128,1024]{1,0:T(8,128)(2,1)S(1)} %fusion.13), channel_id=1, source_target_pairs={{0,16},{8,24},{16,0},{24,8},{1,17},{9,25},{17,1},{25,9},{2,18},{10... | collective-permute-start | bytes 786440 | tf_op jit(solution)/shard_map/ppermute | solution.py:22
  158.4 14.0 %collective-permute-done.11.refs_0_ = bf16[16,128,128]{2,1,0:T(8,128)(2,1)S(1)} collective-permute-done((bf16[16,128,128]{2,1,0:T(8,128)(2,1)}, bf16[16,128,128]{2,1,0:T(8,128)(2,1)S(1)}, u32[]{:S(2)}, u32[]{:S(2)}) %collective-permute-start.11) | collective-permute-done | bytes 524320 | tf_op jit(solution)/shard_map/ppermute | solution.py:390
  176.8 15.0 %shard_map.105 = (bf16[512,2048]{1,0:T(8,128)(2,1)}, f32[512,2048]{1,0:T(8,128)}, f32[512,2048]{1,0:T(8,128)}, f32[1,16,128,128]{3,2,1,0:T(8,128)}, f32[512,128]{1,0:T(8,128)}) custom-call(s32[2]{0:T(128)} %pad_add_fusion.bits_ref, bf16[512,2048]{1,0:T(8,128)(2,1)} %bitcast.119, bf16[512,2048]{1,0:T(8,128)(2,1)} %bitcast.110, bf16[512,2048]{1,0:T(8,128)(2,1)} %bitcast.115, ...), custom_call_target="tpu_custom_call" | custom-call | flops 1879048192 | bytes 10485760 | tf_op jit(solution)/shard_map/pallas_call | solution.py:417
  191.7 15.1 %shard_map.106 = (bf16[512,2048]{1,0:T(8,128)(2,1)}, f32[512,2048]{1,0:T(8,128)}, f32[512,2048]{1,0:T(8,128)}, f32[1,16,128,128]{3,2,1,0:T(8,128)}, f32[512,128]{1,0:T(8,128)}) custom-call(s32[2]{0:T(128)} %pad_add_fusion.bits_ref, bf16[512,2048]{1,0:T(8,128)(2,1)} %bitcast.120, ...), custom_call_target="tpu_custom_call", output_to_operand_aliasing={{0}: (9, {}), {1}: (10, {}), {2}: (11, {}), {3}: (12, {})} | custom-call | flops 1879048192 | bytes 10485760 | tf_op jit(solution)/shard_map/pallas_call | solution.py:417
  207.7 8.6 %shard_map.109 = (bf16[512,2048]{1,0:T(8,128)(2,1)}, bf16[512,2048]{1,0:T(8,128)(2,1)}) custom-call(s32[3]{0:T(128)} %stack.78.shares_ref, bf16[512,2048]{1,0:T(8,128)(2,1)} %bitcast.112, bf16[512,2048]{1,0:T(8,128)(2,1)} %bitcast.117, f32[512,2048]{1,0:T(8,128)} %get-tuple-element.37.gk_ref, f32[512,2048]{1,0:T(8,128)} %get-tuple-element.38.gv_ref, ...), custom_call_target="tpu_custom_call" | custom-call | flops 536870912 | bytes 16777216 | tf_op jit(solution)/shard_map/pallas_call | solution.py:435
  (65 shorter events, 27.9 us)
Async XLA Ops:
  5.4 18.5 %copy-start = (bf16[1,512,2048]{2,1,0:T(8,128)(2,1)S(1)}, bf16[1,512,2048]{2,1,0:T(8,128)(2,1)}, u32[]{:S(2)}) copy-start(bf16[1,512,2048]{2,1,0:T(8,128)(2,1)} %param.11) | copy-start | bytes 6291460
  5.4 14.0 %collective-permute-start.9 = (bf16[16,128,128]{2,1,0:T(8,128)(2,1)}, bf16[16,128,128]{2,1,0:T(8,128)(2,1)S(1)}, u32[]{:S(2)}, u32[]{:S(2)}) collective-permute-start(bf16[16,128,128]{2,1,0:T(8,128)(2,1)} %get-tuple-element.29), channel_id=1, source_target_pairs={{0,8},{8,0},{16,24},{24,16},{1,9},{9,1},{17,25},{25,17},{2,10},{10... | collective-permute-start | bytes 1572872 | tf_op jit(solution)/shard_map/ppermute | solution.py:22
  19.4 19.6 %copy-start.1 = (bf16[16,128,128]{2,1,0:T(8,128)(2,1)}, bf16[16,128,128]{2,1,0:T(8,128)(2,1)S(1)}, u32[]{:S(2)}) copy-start(bf16[16,128,128]{2,1,0:T(8,128)(2,1)S(1)} %collective-permute-done.9.refs_0_) | copy-start | bytes 1572868
  21.7 25.3 %collective-permute-start.10 = (bf16[16,128,128]{2,1,0:T(8,128)(2,1)}, bf16[16,128,128]{2,1,0:T(8,128)(2,1)S(1)}, u32[]{:S(2)}, u32[]{:S(2)}) collective-permute-start(bf16[16,128,128]{2,1,0:T(8,128)(2,1)} %add_convert_fusion.1), channel_id=1, source_target_pairs={{0,16},{8,24},{16,0},{24,8},{1,17},{9,25},{17,1},{25,9},{2,18},{10... | collective-permute-start | bytes 1572872 | tf_op jit(solution)/shard_map/ppermute | solution.py:22
  23.9 34.4 %collective-permute-start.15 = (bf16[512,2048]{1,0:T(8,128)(2,1)S(1)}, bf16[512,2048]{1,0:T(8,128)(2,1)}, u32[]{:S(2)}, u32[]{:S(2)}) collective-permute-start(bf16[512,2048]{1,0:T(8,128)(2,1)S(1)} %bitcast.107), channel_id=1, source_target_pairs={{0,1},{1,0},{2,3},{3,2},{4,5},{5,4},{6,7},{7,6},{8,9},{9,8},{10,11... | collective-permute-start | bytes 6291464 | tf_op jit(solution)/shard_map/ppermute | solution.py:22
  47.0 0.8 copy-start.2
  54.6 5.5 %collective-permute-start.14 = (bf16[512,2048]{1,0:T(8,128)(2,1)}, bf16[512,2048]{1,0:T(8,128)(2,1)}, u32[]{:S(2)}, u32[]{:S(2)}) collective-permute-start(bf16[512,2048]{1,0:T(8,128)(2,1)} %shard_map.110.attn_ref), channel_id=1, source_target_pairs={{0,1},{1,0},{2,3},{3,2},{4,5},{5,4},{6,7},{7,6},{8,9},{9,8},{10,11... | collective-permute-start | bytes 6291464 | tf_op jit(solution)/shard_map/ppermute | solution.py:22
  56.0 25.0 %collective-permute-start = (bf16[256,2048]{1,0:T(8,128)(2,1)}, bf16[256,2048]{1,0:T(8,128)(2,1)S(1)}, u32[]{:S(2)}, u32[]{:S(2)}) collective-permute-start(bf16[256,2048]{1,0:T(8,128)(2,1)} %refs_0_.1), channel_id=1, source_target_pairs={{0,2},{1,3},{2,0},{3,1},{4,6},{5,7},{6,4},{7,5},{8,10},{9,11},{10,... | collective-permute-start | bytes 3145736 | tf_op jit(solution)/shard_map/ppermute | solution.py:22
  57.1 26.0 %collective-permute-start.2 = (bf16[256,2048]{1,0:T(8,128)(2,1)}, bf16[256,2048]{1,0:T(8,128)(2,1)}, u32[]{:S(2)}, u32[]{:S(2)}) collective-permute-start(bf16[256,2048]{1,0:T(8,128)(2,1)} %refs_0_.1), channel_id=1, source_target_pairs={{0,4},{1,5},{2,6},{3,7},{4,0},{5,1},{6,2},{7,3},{8,12},{9,13},{10,... | collective-permute-start | bytes 3145736 | tf_op jit(solution)/shard_map/ppermute | solution.py:22
  66.3 38.0 %collective-permute-start.18 = (bf16[1024,512]{1,0:T(8,128)(2,1)}, bf16[1024,512]{1,0:T(8,128)(2,1)}, u32[]{:S(2)}, u32[]{:S(2)}) collective-permute-start(bf16[1024,512]{1,0:T(8,128)(2,1)} %get-tuple-element.50), channel_id=1, source_target_pairs={{0,4},{1,5},{2,6},{3,7},{4,0},{5,1},{6,2},{7,3},{8,12},{9,13},{10,... | collective-permute-start | bytes 3145736 | tf_op jit(solution)/shard_map/ppermute | solution.py:22
  67.5 39.6 %collective-permute-start.16 = (bf16[1024,512]{1,0:T(8,128)(2,1)}, bf16[1024,512]{1,0:T(8,128)(2,1)}, u32[]{:S(2)}, u32[]{:S(2)}) collective-permute-start(bf16[1024,512]{1,0:T(8,128)(2,1)} %get-tuple-element.48), channel_id=1, source_target_pairs={{0,2},{1,3},{2,0},{3,1},{4,6},{5,7},{6,4},{7,5},{8,10},{9,11},{10,... | collective-permute-start | bytes 3145736 | tf_op jit(solution)/shard_map/ppermute | solution.py:22
  68.7 42.8 %collective-permute-start.8 = (bf16[256,2048]{1,0:T(8,128)(2,1)}, bf16[256,2048]{1,0:T(8,128)(2,1)}, u32[]{:S(2)}, u32[]{:S(2)}) collective-permute-start(bf16[256,2048]{1,0:T(8,128)(2,1)} %refs_0_.1), channel_id=1, source_target_pairs={{0,1},{1,0},{2,3},{3,2},{4,5},{5,4},{6,7},{7,6},{8,9},{9,8},{10,11... | collective-permute-start | bytes 3145736 | tf_op jit(solution)/shard_map/ppermute | solution.py:22
  81.0 30.5 %copy-start.3 = (bf16[256,2048]{1,0:T(8,128)(2,1)}, bf16[256,2048]{1,0:T(8,128)(2,1)S(1)}, u32[]{:S(2)}) copy-start(bf16[256,2048]{1,0:T(8,128)(2,1)S(1)} %collective-permute-done.refs_0_) | copy-start | bytes 3145732
  81.9 33.6 %collective-permute-start.1 = (bf16[128,2048]{1,0:T(8,128)(2,1)}, bf16[128,2048]{1,0:T(8,128)(2,1)}, u32[]{:S(2)}, u32[]{:S(2)}) collective-permute-start(bf16[128,2048]{1,0:T(8,128)(2,1)} %slice.61), channel_id=1, source_target_pairs={{0,4},{1,5},{2,6},{3,7},{4,0},{5,1},{6,2},{7,3},{8,12},{9,13},{10,... | collective-permute-start | bytes 1572872 | tf_op jit(solution)/shard_map/ppermute | solution.py:22
  85.0 37.6 %collective-permute-start.3 = (bf16[128,2048]{1,0:T(8,128)(2,1)}, bf16[128,2048]{1,0:T(8,128)(2,1)}, u32[]{:S(2)}, u32[]{:S(2)}) collective-permute-start(bf16[128,2048]{1,0:T(8,128)(2,1)} %slice.62), channel_id=1, source_target_pairs={{0,2},{1,3},{2,0},{3,1},{4,6},{5,7},{6,4},{7,5},{8,10},{9,11},{10,... | collective-permute-start | bytes 1572872 | tf_op jit(solution)/shard_map/ppermute | solution.py:22
  92.6 14.5 %copy-start.4 = (f32[1024,512]{1,0:T(8,128)S(1)}, f32[1024,512]{1,0:T(8,128)}, u32[]{:S(2)}) copy-start(f32[1024,512]{1,0:T(8,128)} %get-tuple-element.47) | copy-start | bytes 6291460
  106.7 19.3 %collective-permute-start.19 = (bf16[4,128,512]{2,1,0:T(8,128)(2,1)}, bf16[4,128,512]{2,1,0:T(8,128)(2,1)}, u32[]{:S(2)}, u32[]{:S(2)}) collective-permute-start(bf16[4,128,512]{2,1,0:T(8,128)(2,1)} %fusion.10), channel_id=1, source_target_pairs={{0,2},{1,3},{2,0},{3,1},{4,6},{5,7},{6,4},{7,5},{8,10},{9,11},{10,... | collective-permute-start | bytes 1572872 | tf_op jit(solution)/shard_map/ppermute | solution.py:22
  109.1 19.5 %collective-permute-start.17 = (bf16[4,128,512]{2,1,0:T(8,128)(2,1)}, bf16[4,128,512]{2,1,0:T(8,128)(2,1)}, u32[]{:S(2)}, u32[]{:S(2)}) collective-permute-start(bf16[4,128,512]{2,1,0:T(8,128)(2,1)} %fusion.9), channel_id=1, source_target_pairs={{0,4},{1,5},{2,6},{3,7},{4,0},{5,1},{6,2},{7,3},{8,12},{9,13},{10,... | collective-permute-start | bytes 1572872 | tf_op jit(solution)/shard_map/ppermute | solution.py:22
  111.5 19.9 %collective-permute-start.6 = (bf16[256,2048]{1,0:T(8,128)(2,1)S(1)}, bf16[256,2048]{1,0:T(8,128)(2,1)}, u32[]{:S(2)}, u32[]{:S(2)}) collective-permute-start(bf16[256,2048]{1,0:T(8,128)(2,1)S(1)} %collective-permute-done.refs_0_), channel_id=1, source_target_pairs={{0,1},{1,0},{2,3},{3,2},{4,5},{5,4},{6,7},{7,6},{8,9},{9,8},{10,11... | collective-permute-start | bytes 3145736 | tf_op jit(solution)/shard_map/ppermute | solution.py:22
  115.6 15.8 %collective-permute-start.7 = (bf16[256,2048]{1,0:T(8,128)(2,1)}, bf16[256,2048]{1,0:T(8,128)(2,1)}, u32[]{:S(2)}, u32[]{:S(2)}) collective-permute-start(bf16[256,2048]{1,0:T(8,128)(2,1)} %collective-permute-done.2.refs_2_), channel_id=1, source_target_pairs={{0,1},{1,0},{2,3},{3,2},{4,5},{5,4},{6,7},{7,6},{8,9},{9,8},{10,11... | collective-permute-start | bytes 3145736 | tf_op jit(solution)/shard_map/ppermute | solution.py:22
  122.5 16.2 %collective-permute-start.4 = (bf16[128,2048]{1,0:T(8,128)(2,1)}, bf16[128,2048]{1,0:T(8,128)(2,1)S(1)}, u32[]{:S(2)}, u32[]{:S(2)}) collective-permute-start(bf16[128,2048]{1,0:T(8,128)(2,1)} %collective-permute-done.1.refs_0_), channel_id=1, source_target_pairs={{0,1},{1,0},{2,3},{3,2},{4,5},{5,4},{6,7},{7,6},{8,9},{9,8},{10,11... | collective-permute-start | bytes 1572872 | tf_op jit(solution)/shard_map/ppermute | solution.py:22
  126.0 12.7 %collective-permute-start.5 = (bf16[128,2048]{1,0:T(8,128)(2,1)}, bf16[128,2048]{1,0:T(8,128)(2,1)}, u32[]{:S(2)}, u32[]{:S(2)}) collective-permute-start(bf16[128,2048]{1,0:T(8,128)(2,1)} %collective-permute-done.3.refs_1_), channel_id=1, source_target_pairs={{0,1},{1,0},{2,3},{3,2},{4,5},{5,4},{6,7},{7,6},{8,9},{9,8},{10,11... | collective-permute-start | bytes 1572872 | tf_op jit(solution)/shard_map/ppermute | solution.py:22
  131.0 22.4 %collective-permute-start.20 = (bf16[2,128,1024]{2,1,0:T(8,128)(2,1)}, bf16[2,128,1024]{2,1,0:T(8,128)(2,1)}, u32[]{:S(2)}, u32[]{:S(2)}) collective-permute-start(bf16[2,128,1024]{2,1,0:T(8,128)(2,1)} %fusion.11), channel_id=1, source_target_pairs={{0,8},{8,0},{16,24},{24,16},{1,9},{9,1},{17,25},{25,17},{2,10},{10... | collective-permute-start | bytes 1572872 | tf_op jit(solution)/shard_map/ppermute | solution.py:22
  138.7 0.8 copy-start.8
  151.5 20.9 %collective-permute-start.11 = (bf16[16,128,128]{2,1,0:T(8,128)(2,1)}, bf16[16,128,128]{2,1,0:T(8,128)(2,1)S(1)}, u32[]{:S(2)}, u32[]{:S(2)}) collective-permute-start(bf16[16,128,128]{2,1,0:T(8,128)(2,1)} %get-tuple-element.41), channel_id=1, source_target_pairs={{8,0},{24,16},{16,24},{9,1},{25,17},{17,25},{10,2},{26,18},{18,26}... | collective-permute-start | bytes 1572872 | tf_op jit(solution)/shard_map/ppermute | solution.py:390
  153.4 19.0 %copy-start.6 = (f32[16,128,128]{2,1,0:T(8,128)S(1)}, f32[16,128,128]{2,1,0:T(8,128)}, u32[]{:S(2)}) copy-start(f32[16,128,128]{2,1,0:T(8,128)} %get-tuple-element.42) | copy-start | bytes 3145732
  154.7 20.7 %collective-permute-start.21 = (bf16[128,1024]{1,0:T(8,128)(2,1)S(1)}, bf16[128,1024]{1,0:T(8,128)(2,1)S(1)}, u32[]{:S(2)}, u32[]{:S(2)}) collective-permute-start(bf16[128,1024]{1,0:T(8,128)(2,1)S(1)} %fusion.13), channel_id=1, source_target_pairs={{0,16},{8,24},{16,0},{24,8},{1,17},{9,25},{17,1},{25,9},{2,18},{10... | collective-permute-start | bytes 786440 | tf_op jit(solution)/shard_map/ppermute | solution.py:22
  172.4 3.1 %copy-start.5 = (bf16[16,128,128]{2,1,0:T(8,128)(2,1)}, bf16[16,128,128]{2,1,0:T(8,128)(2,1)S(1)}, u32[]{:S(2)}) copy-start(bf16[16,128,128]{2,1,0:T(8,128)(2,1)S(1)} %collective-permute-done.11.refs_0_) | copy-start | bytes 1572868
  173.4 33.5 %collective-permute-start.12 = (bf16[16,128,128]{2,1,0:T(8,128)(2,1)}, bf16[16,128,128]{2,1,0:T(8,128)(2,1)S(1)}, u32[]{:S(2)}, u32[]{:S(2)}) collective-permute-start(bf16[16,128,128]{2,1,0:T(8,128)(2,1)} %add_convert_fusion), channel_id=1, source_target_pairs={{24,8},{25,9},{26,10},{27,11},{28,12},{29,13},{30,14},{31,15}} | collective-permute-start | bytes 1572872 | tf_op jit(solution)/shard_map/ppermute | solution.py:392
  174.1 32.8 %collective-permute-start.13 = (bf16[16,128,128]{2,1,0:T(8,128)(2,1)}, bf16[16,128,128]{2,1,0:T(8,128)(2,1)}, u32[]{:S(2)}, u32[]{:S(2)}) collective-permute-start(bf16[16,128,128]{2,1,0:T(8,128)(2,1)} %add_convert_fusion), channel_id=1, source_target_pairs={{24,0},{25,1},{26,2},{27,3},{28,4},{29,5},{30,6},{31,7}} | collective-permute-start | bytes 1572872 | tf_op jit(solution)/shard_map/ppermute | solution.py:392
  175.5 40.8 %collective-permute-start.22 = (f32[64,1024]{1,0:T(8,128)S(1)}, f32[64,1024]{1,0:T(8,128)S(1)}, u32[]{:S(2)}, u32[]{:S(2)}) collective-permute-start(f32[64,1024]{1,0:T(8,128)S(1)} %get-tuple-element.52), channel_id=1, source_target_pairs={{0,1},{1,0},{2,3},{3,2},{4,5},{5,4},{6,7},{7,6},{8,9},{9,8},{10,11... | collective-permute-start | bytes 786440 | tf_op jit(solution)/shard_map/ppermute | solution.py:22
  206.9 0.8 copy-start.7

commit v2 on v1

v2 whole, which is shorter than its diff:
```python
import functools

import jax
import jax.numpy as jnp
from jax import lax
from jax.experimental import pallas as pl
from jax.experimental.pallas import tpu as pltpu
from jax.sharding import PartitionSpec as P

H = 16
HD = 128
GROUP = 64
LEVELS = 8
HALF = 2 * GROUP
TILE = 4 * GROUP
SCALE = HD ** (-0.5)
EARLY = 60
BF = jnp.bfloat16
F32 = jnp.float32


def swapped(value, axis, mask):
    return lax.ppermute(value, axis, [(source, source ^ mask) for source in range(lax.axis_size(axis))])


def mm(a, b, ca, cb):
    return lax.dot_general(a, b, (((ca,), (cb,)), ((), ())), preferred_element_type=F32)


def call(body, flops, nbytes, vmem=16, **kwargs):
    return pl.pallas_call(
        body,
        cost_estimate=pl.CostEstimate(flops=int(flops), bytes_accessed=int(nbytes), transcendentals=0),
        compiler_params=pltpu.CompilerParams(vmem_limit_bytes=vmem * 1024 * 1024),
        **kwargs,
    )


def level_rows(gain_ref, head, levels):
    return {level: gain_ref[pl.ds(level * H + head, 1), :] for level in levels}


def half_masks():
    source = lax.broadcasted_iota(jnp.int32, (HALF, HALF), 0)
    target = lax.broadcasted_iota(jnp.int32, (HALF, HALF), 1)
    same = (source >= GROUP) == (target >= GROUP)
    return same & (source <= target), (source < GROUP) & (target >= GROUP)


def tile_weight(w, start, own, below):
    first, second = slice(start, start + HALF), slice(start + HALF, start + TILE)
    zero = jnp.zeros((HALF, HALF), F32)

    def corner(at):
        return jnp.where(own, w[0][:, at], jnp.where(below, w[1][:, at], 0.0))

    side = jnp.broadcast_to(w[2][:, second], (HALF, HALF))
    top = jnp.concatenate([corner(first), side], axis=1)
    bottom = jnp.concatenate([zero, corner(second)], axis=1)
    return jnp.concatenate([top, bottom], axis=0)


def far_blocks(seg_len):
    blocks = []
    size, level = TILE, 3
    while size < seg_len:
        for start in range(0, seg_len, 2 * size):
            blocks.append((level, start + size, start, size))
        size, level = 2 * size, level + 1
    return blocks


def states_body(k_ref, v_ref, wide_ref, half_ref, block_ref):
    seg_len = k_ref.shape[0]
    for i in range(wide_ref.shape[0]):
        cols = slice(i * HD, (i + 1) * HD)
        tiles = [
            mm(k_ref[start : start + TILE, cols], v_ref[start : start + TILE, cols], 0, 0)
            for start in range(0, seg_len, TILE)
        ]
        state = sum(tiles[1:], tiles[0])
        wide_ref[i] = state
        half_ref[i] = state.astype(BF)
        for j, (_, _, col, size) in enumerate(far_blocks(seg_len)):
            part = tiles[col // TILE : (col + size) // TILE]
            block_ref[j, i] = sum(part[1:], part[0]).astype(BF)


def intra_body(n_bits, heads, offset, bits_ref, q_ref, k_ref, v_ref, gain_ref, block_ref, *refs):
    out_ref, wq_ref, qt_ref = refs[-3:]
    seg_len = q_ref.shape[0]
    loc_bits = (seg_len // GROUP).bit_length() - 1
    own, below = half_masks()
    for i in range(heads):
        cols = slice(i * HD, (i + 1) * HD)
        w = level_rows(gain_ref, offset + pl.program_id(0) * heads + i, range(loc_bits + 1 + n_bits))
        qt = q_ref[:, cols].T
        qt_ref[cols] = qt
        for b in range(n_bits):
            factor = w[loc_bits + 1 + b] * bits_ref[b].astype(F32)
            at = (i * n_bits + b) * HD
            wq_ref[at : at + HD] = (qt.astype(F32) * factor).astype(BF)
        for start in range(0, seg_len, TILE):
            rows = slice(start, start + TILE)
            scores = mm(k_ref[rows, cols], qt[:, rows], 1, 0) * SCALE
            probs = (scores * tile_weight(w, start, own, below)).astype(BF)
            total = mm(v_ref[rows, cols].T, probs, 1, 0)
            for j, (level, row, _, size) in enumerate(far_blocks(seg_len)):
                if row <= start < row + size:
                    total += mm(block_ref[j, i], qt[:, rows], 0, 0) * (w[level][:, rows] * SCALE)
            out_ref[cols, rows] = total


def attn_body(n_bits, heads, at_ref, wq_ref, intra_ref, *refs):
    far_refs, out_ref = refs[:n_bits], refs[n_bits]
    for i in range(heads):
        cols = slice(i * HD, (i + 1) * HD)
        far = jnp.concatenate([ref[i] for ref in far_refs], axis=0)
        total = intra_ref[cols] + mm(far, wq_ref[i * n_bits * HD : (i + 1) * n_bits * HD], 0, 0) * SCALE
        place = pl.multiple_of((i ^ at_ref[1]) * HD, HD)
        out_ref[pl.ds(place, HD), :] = total.astype(BF)


def weight_body(picks, core_ref, attn_ref, attn2_ref, gx_ref, gx2_ref, gy_ref, gy2_ref, outx_ref, outy_ref):
    del core_ref
    for pick, left, right, out_ref in (
        (picks[0], gx_ref, gx2_ref, outx_ref),
        (picks[1], gy_ref, gy2_ref, outy_ref),
    ):
        total = 0.0
        for ref, grad_ref in ((attn_ref, left), (attn2_ref, right)):
            lhs = jnp.concatenate([ref[p * HD : (p + 1) * HD] for p in pick], axis=0)
            total += mm(lhs, grad_ref[...], 1, 0)
        out_ref[...] = total.astype(out_ref.dtype)


def attn_grad_body(count, at_ref, dout_ref, *refs):
    del at_ref
    out_ref = refs[-1]
    for j in range(count):
        @pl.when(pl.program_id(0) == j)
        def _(j=j):
            out_ref[...] = mm(refs[j][...], dout_ref[...], 1, 1).astype(BF)


def far_grad_body(n_bits, heads, wq_ref, g_ref, half_ref, wide_ref):
    for i in range(heads):
        span = n_bits * HD
        grad = mm(wq_ref[i * span : (i + 1) * span], g_ref[i * HD : (i + 1) * HD], 1, 1) * SCALE
        for b in range(n_bits):
            part = grad[b * HD : (b + 1) * HD]
            half_ref[b, i] = part.astype(BF)
            wide_ref[b, i] = part


def far_grad_four_body(heads, at_ref, wq_ref, g_ref, half_ref, wide_ref):
    for i in range(heads):
        grad = mm(wq_ref[2 * i * HD : 2 * (i + 1) * HD], g_ref[i * HD : (i + 1) * HD], 1, 1) * SCALE
        low, high = grad[:HD], grad[HD:]
        half_ref[i] = jnp.where(at_ref[0] == 3, high, low).astype(BF)
        wide_ref[i] = jnp.where(at_ref[0] == 3, low, high)


def main_body(n_bits, heads, offset, carried, bits_ref, qt_ref, k_ref, v_ref, g_ref, gain_ref, block_ref, *refs):
    far_refs = refs[:n_bits]
    gq_ref, gk_ref, gv_ref, back_ref, gain_grad_ref = refs[n_bits + carried :]
    seg_len = k_ref.shape[0]
    loc_bits = (seg_len // GROUP).bit_length() - 1
    own, below = half_masks()

    def down(x):
        return jnp.sum(x, axis=0, keepdims=True)

    for i in range(heads):
        head = offset + pl.program_id(0) * heads + i
        cols = slice(i * HD, (i + 1) * HD)
        w = level_rows(gain_ref, head, range(loc_bits + 1 + n_bits))
        far = jnp.concatenate([ref[i] for ref in far_refs], axis=0)

        gain_grad_ref[i] = jnp.zeros((LEVELS, seg_len), F32)

        def put(tokens, row, level, i=i):
            gain_grad_ref[i, level : level + 1, tokens] = row

        for start in range(0, seg_len, TILE):
            rows = slice(start, start + TILE)
            first, second = slice(start, start + HALF), slice(start + HALF, start + TILE)
            qt, gt = qt_ref[cols, rows], g_ref[cols, rows]
            qt_wide = qt.astype(F32)
            back = mm(far, gt, 1, 0)
            total = jnp.zeros((HD, TILE), F32)
            for b in range(n_bits):
                term = back[b * HD : (b + 1) * HD]
                bit = bits_ref[b].astype(F32)
                put(rows, down(qt_wide * term) * (SCALE * bit), loc_bits + 1 + b)
                total += term * (w[loc_bits + 1 + b][:, rows] * bit)
            for j, (level, row, _, size) in enumerate(far_blocks(seg_len)):
                if row <= start < row + size:
                    term = mm(block_ref[j, i], gt, 1, 0)
                    put(rows, down(qt_wide * term) * SCALE, level)
                    total += term * w[level][:, rows]
            weight = tile_weight(w, start, own, below)
            scores = mm(k_ref[rows, cols], qt, 1, 0) * SCALE
            prob_grad = mm(v_ref[rows, cols], gt, 1, 0)
            energy = scores * prob_grad
            for half, at in ((first, 0), (second, HALF)):
                corner = energy[at : at + HALF, at : at + HALF]
                put(half, down(jnp.where(own, corner, 0.0)), 0)
                put(half, down(jnp.where(below, corner, 0.0)), 1)
            put(second, down(energy[:HALF, HALF:]), 2)
            probs = (scores * weight).astype(BF)
            score_grad = (prob_grad * weight).astype(BF)
            total += mm(k_ref[rows, cols].T, score_grad, 1, 0)
            gq_ref[rows, cols] = (total * SCALE).astype(BF).T
            gk_ref[cols, rows] = mm(qt, score_grad, 1, 1) * SCALE
            gv_ref[cols, rows] = mm(gt, probs, 1, 1)
        for j, (level, row, _, size) in enumerate(far_blocks(seg_len)):
            rows = slice(row, row + size)
            weighted = (qt_ref[cols, rows].astype(F32) * w[level][:, rows]).astype(BF)
            back_ref[j, i] = mm(weighted, g_ref[cols, rows], 1, 1) * SCALE


def final_body(heads, gates, bits_ref, k_ref, v_ref, gk_ref, gv_ref, back_ref, *refs):
    got_refs, (key_ref, value_ref) = refs[:-3], refs[-2:]
    seg_len = k_ref.shape[0]
    for i in range(heads):
        cols = slice(i * HD, (i + 1) * HD)
        state = jnp.zeros((HD, HD), F32)
        for b, ref in enumerate(got_refs):
            part = ref[i].astype(F32)
            for bit in gates[b]:
                part = part * (1 - bits_ref[bit]).astype(F32)
            state += part
        for start in range(0, seg_len, TILE):
            rows = slice(start, start + TILE)
            here = state
            for j, (_, _, col, size) in enumerate(far_blocks(seg_len)):
                if col <= start < col + size:
                    here = here + back_ref[j, i]
            half = here.astype(BF)
            key = gk_ref[cols, rows] + mm(half, v_ref[rows, cols], 1, 1)
            value = gv_ref[cols, rows] + mm(half, k_ref[rows, cols], 0, 1)
            key_ref[rows, cols] = key.astype(BF).T
            value_ref[rows, cols] = value.astype(BF).T


def sds(shape, dtype):
    return jax.ShapeDtypeStruct(shape, dtype)


def local(queries, keys, values, level_gain, out_weight, out_grad):
    outs = step(queries[0], keys[0], values[0], level_gain[0], out_weight, out_grad[0])
    return tuple(x[None] for x in outs[:4]) + (outs[4],)


def is_fast(seq_count, batch_count):
    return batch_count == 8 and seq_count * batch_count == 2 * H


def step(q, k, v, gain, out_weight, dout):
    seg_len, width = q.shape
    seq_count, batch_count = lax.axis_size("seq"), lax.axis_size("batch")
    n_bits = seq_count.bit_length() - 1
    seg_index, batch_index = lax.axis_index("seq"), lax.axis_index("batch")
    bits = jnp.stack([seg_index >> b & 1 for b in range(n_bits)]).astype(jnp.int32)
    fast = is_fast(seq_count, batch_count)
    prefetch = pltpu.PrefetchScalarGridSpec
    tok_bytes = seg_len * width * 2
    head_flops = 2 * seg_len * HD * HD * H
    n_blocks = len(far_blocks(seg_len))
    mats = (H, HD, HD)

    def cols(heads, scale=1):
        return pl.BlockSpec((seg_len, heads * HD * scale), lambda h, *_: (0, h))

    def turned(heads, scale=1):
        return pl.BlockSpec((heads * HD * scale, seg_len), lambda h, *_: (h, 0))

    def mat(heads):
        return pl.BlockSpec((heads, HD, HD), lambda h, *_: (h, 0, 0))

    def stack(count, heads):
        return pl.BlockSpec((count, heads, HD, HD), lambda h, *_: (0, h, 0, 0))

    whole_gain = pl.BlockSpec((LEVELS * H, seg_len), lambda h, *_: (0, 0))
    gain = gain.T

    state_wide, state_half, blocks = call(
        states_body, head_flops, 2 * tok_bytes, EARLY,
        out_shape=(sds(mats, F32), sds(mats, BF), sds((n_blocks,) + mats, BF)),
        grid=(H // 4,), in_specs=[cols(4), cols(4)],
        out_specs=(mat(4), mat(4), stack(n_blocks, 4)),
    )(k, v)
    fars = []
    running_wide, running = state_wide, state_half
    for b in range(n_bits):
        received = swapped(running, "seq", 1 << b)
        fars.append(received)
        if b + 1 < n_bits:
            running_wide = running_wide + received.astype(F32)
            running = running_wide.astype(BF)

    if fast:
        pieces = {0: out_weight}
        dout_pair = swapped(dout, "batch", 1)
        pieces[2] = swapped(out_weight, "batch", 2)
        pieces[4] = swapped(out_weight, "batch", 4)
        pieces[1] = swapped(out_weight, "batch", 1)
        pieces[3] = swapped(pieces[2], "batch", 1)
        pieces[5] = swapped(pieces[4], "batch", 1)
        pieces[6] = swapped(out_weight, "batch", 6)
        pieces[7] = swapped(pieces[6], "batch", 1)
        stages = [[(pieces[m], batch_index ^ m) for m in group] for group in ((0, 1), (2, 4, 3, 5), (6, 7))]
        g = None
        for stage in stages:
            count, piece_rows = len(stage), stage[0][0].shape[0]
            index = jnp.stack([at for _, at in stage]).astype(jnp.int32)
            arrays = [array for array, _ in stage]
            extra = [] if g is None else [g]
            g = call(
                functools.partial(attn_grad_body, count),
                2 * seg_len * width * piece_rows * count, tok_bytes + count * piece_rows * (width + seg_len) * 2, 30,
                out_shape=pltpu.HBM((width, seg_len), BF),
                grid_spec=prefetch(
                    num_scalar_prefetch=1, grid=(count,),
                    in_specs=[pl.BlockSpec((seg_len, width), lambda j, at: (0, 0))]
                    + [pl.BlockSpec((piece_rows, width), lambda j, at: (0, 0))] * count
                    + [pl.BlockSpec(memory_space=pl.ANY)] * len(extra),
                    out_specs=pl.BlockSpec((piece_rows, seg_len), lambda j, at: (at[j], 0)),
                ),
                input_output_aliases={} if g is None else {2 + count: 0},
            )(index, dout, *arrays, *extra)
    else:
        gathered = lax.all_gather(out_weight, "batch", axis=0, tiled=True)
        g = mm(gathered, dout, 1, 1).astype(BF)

    formed = []
    for part in range(2):
        first = part * (H // 8)
        four = pl.BlockSpec((seg_len, 4 * HD), lambda h, *_, first=first: (0, h + first))
        four_turned = pl.BlockSpec((4 * HD, seg_len), lambda h, *_, first=first: (h + first, 0))
        four_wide = pl.BlockSpec((4 * HD * n_bits, seg_len), lambda h, *_, first=first: (h + first, 0))
        four_blocks = pl.BlockSpec((n_blocks, 4, HD, HD), lambda h, *_, first=first: (0, h + first, 0, 0))
        formed = call(
            functools.partial(intra_body, n_bits, 4, first * 4),
            2 * seg_len * TILE * width, 5 * tok_bytes, EARLY,
            out_shape=(sds((width, seg_len), F32), sds((n_bits * width, seg_len), BF), sds((width, seg_len), BF)),
            grid_spec=prefetch(
                num_scalar_prefetch=1, grid=(H // 8,),
                in_specs=[four, four, four, whole_gain, four_blocks]
                + [pl.BlockSpec(memory_space=pl.ANY)] * len(formed),
                out_specs=(four_turned, four_wide, four_turned),
            ),
            input_output_aliases={6 + i: i for i in range(3)} if formed else {},
        )(bits, q, k, v, gain, blocks, *formed)
    intra, wq, qt = formed

    at = jnp.stack([seg_index, batch_index >> 1]).astype(jnp.int32)
    if not fast:
        at = jnp.zeros_like(at)
    attn = call(
        functools.partial(attn_body, n_bits, 4), head_flops * n_bits, 5 * tok_bytes,
        out_shape=sds((width, seg_len), BF),
        grid_spec=prefetch(
            num_scalar_prefetch=1, grid=(H // 4,),
            in_specs=[
                pl.BlockSpec((4 * HD * n_bits, seg_len), lambda j, a: (j ^ a[0], 0)),
                pl.BlockSpec((4 * HD, seg_len), lambda j, a: (j ^ a[0], 0)),
            ]
            + [pl.BlockSpec((4, HD, HD), lambda j, a: (j ^ a[0], 0, 0))] * n_bits,
            out_specs=pl.BlockSpec((4 * HD, seg_len), lambda j, a: (j, 0)),
        ),
    )(at, wq, intra, *fars)

    if fast:
        weight_grad = reduce_weight(attn, dout, dout_pair, batch_index, seq_count)
    else:
        weight_grad = lax.psum_scatter(
            mm(attn, dout, 1, 0), ("seq", "batch"), scatter_dimension=0, tiled=True
        )

    if fast:
        far_half, far_wide = call(
            functools.partial(far_grad_four_body, 4), head_flops * n_bits, 4 * tok_bytes,
            out_shape=(sds(mats, BF), sds(mats, F32)),
            grid_spec=prefetch(
                num_scalar_prefetch=1, grid=(H // 4,),
                in_specs=[turned(4, n_bits), turned(4)], out_specs=(mat(4), mat(4)),
            ),
        )(seg_index.astype(jnp.int32)[None], wq, g)
        near = lax.ppermute(far_half, "seq", [(1, 0), (3, 2)])
        both = (far_wide + near.astype(F32)).astype(BF)
        got = [near, lax.ppermute(both, "seq", [(2, 0)]), lax.ppermute(both, "seq", [(2, 1), (3, 2)])]
        gates = ((0, 1), (), ())
    else:
        far_half, far_wide = call(
            functools.partial(far_grad_body, n_bits, 4), head_flops * n_bits, 4 * tok_bytes,
            out_shape=(sds((n_bits,) + mats, BF), sds((n_bits,) + mats, F32)),
            grid=(H // 4,), in_specs=[turned(4, n_bits), turned(4)],
            out_specs=(stack(n_bits, 4),) * 2,
        )(wq, g)
        got = []
        pending_half, pending_wide = far_half, far_wide
        for b in range(n_bits):
            received = swapped(pending_half, "seq", 1 << b)
            got.append(received[0])
            if b + 1 < n_bits:
                pending_wide = pending_wide[1:] + received[1:].astype(F32)
                pending_half = pending_wide.astype(BF)
        gates = tuple((b,) for b in range(n_bits))

    done = []
    bounds = (0, H // 8, 3 * H // 8, H // 2)
    for first, last in zip(bounds, bounds[1:]):
        two = pl.BlockSpec((seg_len, 2 * HD), lambda h, *_, first=first: (0, h + first))
        two_turned = pl.BlockSpec((2 * HD, seg_len), lambda h, *_, first=first: (h + first, 0))
        two_mats = pl.BlockSpec((2, HD, HD), lambda h, *_, first=first: (h + first, 0, 0))
        two_blocks = pl.BlockSpec((n_blocks, 2, HD, HD), lambda h, *_, first=first: (0, h + first, 0, 0))
        two_levels = pl.BlockSpec((2, LEVELS, seg_len), lambda h, *_, first=first: (h + first, 0, 0))
        done = call(
            functools.partial(main_body, n_bits, 2, first * 2, len(done)),
            (5 * seg_len * TILE * width + head_flops * 2) * (last - first) // 4, 5 * tok_bytes * (last - first) // 4,
            out_shape=(
                sds((seg_len, width), BF), pltpu.HBM((width, seg_len), F32), pltpu.HBM((width, seg_len), F32),
                pltpu.HBM((n_blocks,) + mats, F32), sds((H, LEVELS, seg_len), F32),
            ),
            grid_spec=prefetch(
                num_scalar_prefetch=1, grid=(last - first,),
                in_specs=[two_turned, two, two, two_turned, whole_gain, two_blocks] + [two_mats] * n_bits
                + ([pl.BlockSpec(memory_space=pl.ANY)] * 5 if done else []),
                out_specs=(two, two_turned, two_turned, two_blocks, two_levels),
            ),
            input_output_aliases={7 + n_bits + i: i for i in range(5)} if done else {},
        )(bits, qt, k, v, g, gain, blocks, *fars, *done)
    query_grad, key_in, value_in, back, gain_grad = done

    gain_grad = gain_grad.transpose(2, 1, 0).reshape(seg_len, LEVELS * H)
    key_grad, value_grad = call(
        functools.partial(final_body, 4, gates), 2 * head_flops, 8 * tok_bytes, 56,
        out_shape=(sds((seg_len, width), BF),) * 2,
        grid_spec=prefetch(
            num_scalar_prefetch=1, grid=(H // 4,),
            in_specs=[cols(4)] * 2 + [turned(4)] * 2 + [stack(n_blocks, 4)] + [mat(4)] * len(got)
            + [pl.BlockSpec(memory_space=pl.ANY)],
            out_specs=(cols(4), cols(4)),
        ),
    )(bits, k, v, key_in, value_in, back, *got, gain_grad)
    return query_grad, key_grad, value_grad, gain_grad, weight_grad


def reduce_weight(attn, dout, dout_pair, batch_index, seq_count):
    width, seg_len = attn.shape
    quarter = width // 4
    core = batch_index & 1
    attn_pair = swapped(attn, "batch", 1)
    half = core.astype(jnp.int32)[None]

    def products(picks, dtype):
        lhs = pl.BlockSpec((4 * HD, seg_len), lambda j, c: (j, 0))
        grads = [pl.BlockSpec((seg_len, quarter), lambda j, c, n=n: (0, 2 * c[0] + n)) for n in (0, 0, 1, 1)]
        out = pl.BlockSpec((2 * HD, quarter), lambda j, c: (j, 0))
        return call(
            functools.partial(weight_body, picks), 4 * seg_len * width * quarter,
            2 * seg_len * (width + 2 * quarter) * 2 + width * quarter * 2,
            out_shape=(sds((width // 2, quarter), dtype),) * 2,
            grid_spec=pltpu.PrefetchScalarGridSpec(
                num_scalar_prefetch=1, grid=(width // (4 * HD),),
                in_specs=[lhs, lhs] + grads, out_specs=(out, out),
            ),
        )(half, attn, attn_pair, dout, dout_pair, dout, dout_pair)

    send_x, send_y = products(((1, 3), (2, 3)), BF)
    got_x = swapped(send_x, "batch", 2)
    got_y = swapped(send_y, "batch", 4)
    keep_x, keep_y = products(((0, 2), (0, 1)), F32)

    def pick(array, which):
        return array.reshape(seq_count, 2, HD, quarter)[:, which].astype(F32)

    send_xy = (pick(keep_x, 1) + pick(got_x, 1)).astype(BF)
    send_yx = (pick(keep_y, 1) + pick(got_y, 1)).astype(BF)
    got_xy = swapped(send_xy, "batch", 4)
    got_yx = swapped(send_yx, "batch", 2)
    left = pick(keep_x, 0) + pick(got_x, 0) + got_xy.astype(F32)
    right = pick(keep_y, 0) + pick(got_y, 0) + got_yx.astype(F32)
    total = jnp.concatenate([left, right], axis=2).reshape(2, 2, HD, width // 2)
    got_z = swapped(total[:, 1].astype(BF), "seq", 1)
    got_zz = swapped((total[1, 0] + got_z[1].astype(F32)).astype(BF), "seq", 2)
    mine = total[0, 0] + got_z[0].astype(F32) + got_zz.astype(F32)
    rows = mine.shape[0] // 2
    other = swapped(lax.dynamic_slice_in_dim(mine, (1 - core) * rows, rows, 0), "batch", 1)
    own = lax.dynamic_slice_in_dim(mine, core * rows, rows, 0)
    return jnp.where(
        core == 0, jnp.concatenate([own, other], axis=1), jnp.concatenate([other, own], axis=1)
    )


def solution(mesh):
    row = P("batch", "seq", None)
    return jax.shard_map(
        local,
        mesh=mesh,
        in_specs=(row, row, row, row, P("batch", None), row),
        out_specs=(row, row, row, row, P(("seq", "batch"), None)),
        check_vma=False,
    )
```

time: 219 us -> 231 us (1.055)
  starting transfers between devices: 30.7 us -> 54.7 us
  Pallas kernels: 99.9 us -> 76 us
  local copies, waits for them, and re-layouts: 6.69 us -> 17.5 us
    ppermute x20 -> x18, starting transfers between devices: 27.4 us -> 50.4 us  [swapped(): lax.ppermute(value, axis, [(source, source ^ mask) for source in range(la...]
    ppermute x20 -> x18, waiting for transfers between devices: 48.7 us -> 61.3 us  [swapped(): lax.ppermute(value, axis, [(source, source ^ mask) for source in range(la...]
    unnamed x18 -> x50, local copies, waits for them, and re-layouts: 2.41 us -> 14.7 us
    ppermute x3, waiting for transfers between devices: 14 us -> 1.75 us  [the longest x1 1.74 us: step(): lax.ppermute(both, 'seq', [(2, 0)])]
    pallas_call x5 -> x7, Pallas kernels: 56.1 us -> 44.8 us  [the longest x3 17.5 us: step(): call(functools.partial(main_body, n_bits, 2, first * 2, len(done)), (5 *...]
    pallas_call x3, Pallas kernels: 19 us -> 14.5 us  [step(): call(functools.partial(attn_grad_body, count), 2 * seg_len * width * piec...]
    pallas_call x1, Pallas kernels: 6.77 us -> 3.21 us  [step(): call(functools.partial(attn_body, n_bits, 4), head_flops * n_bits, 5 * to...]
    slice x2 -> x0, local copies, waits for them, and re-layouts: 2.79 us -> none  [the longest x1 1.89 us: step(): diag_high = swapped(pieces[4][rows // 2:], 'batch', 2)]
  transfers between devices with their start and end apart: 23 -> 21, of which waited for: 8 -> 8; matrix products, arithmetic and copies ran while one was open for 8% -> 7% of each run, Pallas kernels for 44% -> 29%
where the time goes in v2:
time: 231 us; the launch traced here: 228 us
  Pallas kernels  76 us (33%)
  waiting for transfers between devices  63 us (27%)
  starting transfers between devices  54.7 us (24%)
  local copies, waits for them, and re-layouts  17.5 us (8%)
  other arithmetic  15.6 us (7%)
    ppermute x18, waiting for transfers between devices, swapped(): lax.ppermute(value, axis, [(source, source ^ mask) for source in range(la...  61.3 us
    ppermute x18, starting transfers between devices, swapped(): lax.ppermute(value, axis, [(source, source ^ mask) for source in range(la...  50.4 us
    pallas_call x3, Pallas kernels, step(): call(functools.partial(main_body, n_bits, 2, first * 2, len(done)), (5 *...  17.5 us
    unnamed x50, local copies, waits for them, and re-layouts  14.7 us
    pallas_call x3, Pallas kernels, step(): call(functools.partial(attn_grad_body, count), 2 * seg_len * width * piec...  14.5 us
    pallas_call x2, Pallas kernels, step(): call(functools.partial(intra_body, n_bits, 4, first * 4), 2 * seg_len * T...  13.5 us
    pallas_call x2, Pallas kernels, products(): call(functools.partial(weight_body, picks), 4 * seg_len * width * quarter...  10.8 us
    pallas_call x1, Pallas kernels, step(): call(functools.partial(final_body, 4, gates), 2 * head_flops, 8 * tok_byt...  8.89 us
  transfers between devices with their start and end apart: 21, of which 8 were waited for; matrix products, arithmetic and copies ran while one was open for 7% of the time, Pallas kernels for 29%

profile of v2, /device:TPU:1, one launch (start us, length us, event | category | flops | bytes accessed | tf_op | source)
XLA Modules:
  0.0 227.7 jit_solution(12917471355522208164)
XLA Ops:
  0.6 4.8 %shard_map.101 = (f32[16,128,128]{2,1,0:T(8,128)}, bf16[16,128,128]{2,1,0:T(8,128)(2,1)}, bf16[1,16,128,128]{3,2,1,0:T(8,128)(2,1)}) custom-call(bf16[512,2048]{1,0:T(8,128)(2,1)} %bitcast.103, bf16[512,2048]{1,0:T(8,128)(2,1)} %bitcast.110), custom_call_target="tpu_custom_call" | custom-call | flops 268435456 | bytes 4194304 | tf_op jit(solution)/shard_map/pallas_call | solution.py:288
  5.5 2.1 collective-permute-start.7
  7.6 11.8 %collective-permute-done.7.refs_0_ = bf16[16,128,128]{2,1,0:T(8,128)(2,1)S(1)} collective-permute-done((bf16[16,128,128]{2,1,0:T(8,128)(2,1)}, bf16[16,128,128]{2,1,0:T(8,128)(2,1)S(1)}, u32[]{:S(2)}, u32[]{:S(2)}) %collective-permute-start.7) | collective-permute-done | bytes 524320 | tf_op jit(solution)/shard_map/ppermute | solution.py:23
  19.4 2.2 add_convert_fusion.1
  21.6 2.2 collective-permute-start.8
  27.0 6.8 %shard_map.102 = (f32[2048,512]{1,0:T(8,128)}, bf16[4096,512]{1,0:T(8,128)(2,1)}, bf16[2048,512]{1,0:T(8,128)(2,1)}) custom-call(s32[2]{0:T(128)} %pad_add_fusion.bits_ref, bf16[512,2048]{1,0:T(8,128)(2,1)} %bitcast.135, bf16[512,2048]{1,0:T(8,128)(2,1)} %bitcast.104, bf16[512,2048]{1,0:T(8,128)(2,1)} %bitcast.111, f32[128,512]{1,0:T(8,128)} %bitcast.125, ...), custom_call_target="tpu_custom_call" | custom-call | flops 536870912 | bytes 10485760 | tf_op jit(solution)/shard_map/pallas_call | solution.py:344
  33.9 6.7 %shard_map.103 = (f32[2048,512]{1,0:T(8,128)}, bf16[4096,512]{1,0:T(8,128)(2,1)}, bf16[2048,512]{1,0:T(8,128)(2,1)}) custom-call(s32[2]{0:T(128)} %pad_add_fusion.bits_ref, bf16[512,2048]{1,0:T(8,128)(2,1)} %bitcast.136, bf16[512,2048]{1,0:T(8,128)(2,1)} %bitcast.105, ...), custom_call_target="tpu_custom_call", output_to_operand_aliasing={{0}: (6, {}), {1}: (7, {}), {2}: (8, {})} | custom-call | flops 536870912 | bytes 10485760 | tf_op jit(solution)/shard_map/pallas_call | solution.py:344
  40.6 6.2 %collective-permute-done.8.refs_1_ = bf16[16,128,128]{2,1,0:T(8,128)(2,1)S(1)} collective-permute-done((bf16[16,128,128]{2,1,0:T(8,128)(2,1)}, bf16[16,128,128]{2,1,0:T(8,128)(2,1)S(1)}, u32[]{:S(2)}, u32[]{:S(2)}) %collective-permute-start.8) | collective-permute-done | bytes 524320 | tf_op jit(solution)/shard_map/ppermute | solution.py:23
  46.8 2.4 %copy-done.5 = bf16[4096,512]{1,0:T(8,128)(2,1)S(1)} copy-done((bf16[4096,512]{1,0:T(8,128)(2,1)S(1)}, bf16[4096,512]{1,0:T(8,128)(2,1)}, u32[]{:S(2)}) %copy-start.5) | copy-done | bytes 4194328
  49.2 2.2 copy-done.8
  51.4 3.2 %shard_map.112.attn_ref = bf16[2048,512]{1,0:T(8,128)(2,1)} custom-call(s32[2]{0:T(128)S(1)} %pad_add_fusion.4.at_ref, bf16[4096,512]{1,0:T(8,128)(2,1)S(1)} %copy-done.5, f32[2048,512]{1,0:T(8,128)S(1)} %copy-done.8, bf16[16,128,128]{2,1,0:T(8,128)(2,1)S(1)} %collective-permute-done.7.refs_0_, bf16[16,128,128]{2,1,0:T(8,128)(2,1)S(1)} %collective-permute-done.8.refs_1_), custom_call_target="tpu_custom_call" | custom-call | flops 536870912 | bytes 10485760 | tf_op jit(solution)/shard_map/pallas_call | solution.py:361
  56.0 4.1 %collective-permute-done.12.attn2_ref = bf16[2048,512]{1,0:T(8,128)(2,1)} collective-permute-done((bf16[2048,512]{1,0:T(8,128)(2,1)}, bf16[2048,512]{1,0:T(8,128)(2,1)}, u32[]{:S(2)}, u32[]{:S(2)}) %collective-permute-start.12) | collective-permute-done | bytes 2097184 | tf_op jit(solution)/shard_map/ppermute | solution.py:23
  60.1 5.8 %shard_map.114 = (bf16[1024,512]{1,0:T(8,128)(2,1)}, bf16[1024,512]{1,0:T(8,128)(2,1)}) custom-call(s32[1]{0:T(128)} %bitcast.24.core_ref, bf16[2048,512]{1,0:T(8,128)(2,1)} %shard_map.112.attn_ref, bf16[2048,512]{1,0:T(8,128)(2,1)} %collective-permute-done.12.attn2_ref, bf16[512,2048]{1,0:T(8,128)(2,1)S(1)} %bitcast.118, ...), custom_call_target="tpu_custom_call" | custom-call | flops 2147483648 | bytes 8388608 | tf_op jit(solution)/shard_map/pallas_call | solution.py:462
  68.9 2.1 collective-permute-start
  70.9 19.7 %collective-permute-done.14 = bf16[1024,512]{1,0:T(8,128)(2,1)} collective-permute-done((bf16[1024,512]{1,0:T(8,128)(2,1)}, bf16[1024,512]{1,0:T(8,128)(2,1)}, u32[]{:S(2)}, u32[]{:S(2)}) %collective-permute-start.14) | collective-permute-done | bytes 1048608 | tf_op jit(solution)/shard_map/ppermute | solution.py:23
  90.6 2.1 collective-permute-start.6
  92.7 5.0 %shard_map.113 = (f32[1024,512]{1,0:T(8,128)S(1)}, f32[1024,512]{1,0:T(8,128)S(1)}) custom-call(s32[1]{0:T(128)} %bitcast.24.core_ref, bf16[2048,512]{1,0:T(8,128)(2,1)} %shard_map.112.attn_ref, bf16[2048,512]{1,0:T(8,128)(2,1)} %collective-permute-done.12.attn2_ref, bf16[512,2048]{1,0:T(8,128)(2,1)S(1)} %bitcast.120, ...), custom_call_target="tpu_custom_call" | custom-call | flops 2147483648 | bytes 8388608 | tf_op jit(solution)/shard_map/pallas_call | solution.py:462
  100.6 2.0 fusion.10
  102.6 11.3 %collective-permute-done.3.refs_1_ = bf16[256,2048]{1,0:T(8,128)(2,1)} collective-permute-done((bf16[256,2048]{1,0:T(8,128)(2,1)}, bf16[256,2048]{1,0:T(8,128)(2,1)}, u32[]{:S(2)}, u32[]{:S(2)}) %collective-permute-start.3) | collective-permute-done | bytes 1048608 | tf_op jit(solution)/shard_map/ppermute | solution.py:23
  114.4 25.1 %collective-permute-start.5 = (bf16[256,2048]{1,0:T(8,128)(2,1)}, bf16[256,2048]{1,0:T(8,128)(2,1)S(1)}, u32[]{:S(2)}, u32[]{:S(2)}) collective-permute-start(bf16[256,2048]{1,0:T(8,128)(2,1)} %collective-permute-done.3.refs_1_), channel_id=1, source_target_pairs={{0,1},{1,0},{2,3},{3,2},{4,5},{5,4},{6,7},{7,6},{8,9},{9,8},{10,11... | collective-permute-start | bytes 3145736 | tf_op jit(solution)/shard_map/ppermute | solution.py:23
  140.0 4.3 %shard_map.104.refs_4_ = bf16[2048,512]{1,0:T(8,128)(2,1)} custom-call(s32[2]{0:T(128)S(1)} %pad_add_fusion.3.at_ref, bf16[512,2048]{1,0:T(8,128)(2,1)S(1)} %bitcast.122, bf16[256,2048]{1,0:T(8,128)(2,1)} %refs_0_.1, bf16[256,2048]{1,0:T(8,128)(2,1)} %collective-permute-done.6.refs_1_), custom_call_target="tpu_custom_call" | custom-call | flops 1073741824 | bytes 4718592 | tf_op jit(solution)/shard_map/pallas_call | solution.py:320
  144.3 3.3 %collective-permute-done.15 = bf16[4,128,512]{2,1,0:T(8,128)(2,1)} collective-permute-done((bf16[4,128,512]{2,1,0:T(8,128)(2,1)S(1)}, bf16[4,128,512]{2,1,0:T(8,128)(2,1)}, u32[]{:S(2)}, u32[]{:S(2)}) %collective-permute-start.15) | collective-permute-done | bytes 524320 | tf_op jit(solution)/shard_map/ppermute | solution.py:23
  152.2 5.9 %shard_map.105.refs_2_ = bf16[2048,512]{1,0:T(8,128)(2,1)} custom-call(s32[4]{0:T(128)S(1)} %pad_add_fusion.2.at_ref, bf16[512,2048]{1,0:T(8,128)(2,1)S(1)} %bitcast.123, bf16[256,2048]{1,0:T(8,128)(2,1)} %collective-permute-done.2.refs_0_, bf16[256,2048]{1,0:T(8,128)(2,1)} %collective-permute-done.3.refs_1_, ...), custom_call_target="tpu_custom_call", output_to_operand_aliasing={{}: (6, {})} | custom-call | flops 2147483648 | bytes 7340032 | tf_op jit(solution)/shard_map/pallas_call | solution.py:320
  158.1 4.3 %shard_map.106.g_ref = bf16[2048,512]{1,0:T(8,128)(2,1)} custom-call(s32[2]{0:T(128)S(1)} %pad_add_fusion.1.at_ref, bf16[512,2048]{1,0:T(8,128)(2,1)S(1)} %bitcast.124, bf16[256,2048]{1,0:T(8,128)(2,1)} %collective-permute-done.refs_0_, bf16[256,2048]{1,0:T(8,128)(2,1)S(1)} %collective-permute-done.1.refs_1_, ...), custom_call_target="tpu_custom_call", output_to_operand_aliasing={{}: (4, {})} | custom-call | flops 1073741824 | bytes 4718592 | tf_op jit(solution)/shard_map/pallas_call | solution.py:320
  164.0 2.7 %shard_map.110 = (bf16[16,128,128]{2,1,0:T(8,128)(2,1)}, f32[16,128,128]{2,1,0:T(8,128)S(1)}) custom-call(s32[1]{0:T(128)} %bitcast.18.at_ref, bf16[4096,512]{1,0:T(8,128)(2,1)S(1)} %copy-done.6, bf16[2048,512]{1,0:T(8,128)(2,1)S(1)} %copy-done.3), custom_call_target="tpu_custom_call" | custom-call | flops 536870912 | bytes 8388608 | tf_op jit(solution)/shard_map/pallas_call | solution.py:383
  175.0 4.8 %shard_map.107 = (bf16[512,2048]{1,0:T(8,128)(2,1)}, f32[2048,512]{1,0:T(8,128)}, f32[2048,512]{1,0:T(8,128)}, f32[1,16,128,128]{3,2,1,0:T(8,128)}, f32[16,8,512]{2,1,0:T(8,128)S(1)}) custom-call(s32[2]{0:T(128)S(1)} %copy-done.19, bf16[2048,512]{1,0:T(8,128)(2,1)S(1)} %copy-done.7, bf16[512,2048]{1,0:T(8,128)(2,1)S(1)} %bitcast.107, ...), custom_call_target="tpu_custom_call" | custom-call | flops 939524096 | bytes 5242880 | tf_op jit(solution)/shard_map/pallas_call | solution.py:420
  180.8 3.0 %collective-permute-start.19 = (bf16[128,1024]{1,0:T(8,128)(2,1)S(1)}, bf16[128,1024]{1,0:T(8,128)(2,1)S(1)}, u32[]{:S(2)}, u32[]{:S(2)}) collective-permute-start(bf16[128,1024]{1,0:T(8,128)(2,1)S(1)} %fusion.13), channel_id=1, source_target_pairs={{0,16},{8,24},{16,0},{24,8},{1,17},{9,25},{17,1},{25,9},{2,18},{10... | collective-permute-start | bytes 786440 | tf_op jit(solution)/shard_map/ppermute | solution.py:23
  188.6 4.9 %collective-permute-done.19 = bf16[128,1024]{1,0:T(8,128)(2,1)S(1)} collective-permute-done((bf16[128,1024]{1,0:T(8,128)(2,1)S(1)}, bf16[128,1024]{1,0:T(8,128)(2,1)S(1)}, u32[]{:S(2)}, u32[]{:S(2)}) %collective-permute-start.19) | collective-permute-done | bytes 262176 | tf_op jit(solution)/shard_map/ppermute | solution.py:23
  195.4 5.2 %collective-permute-start.20 = (f32[64,1024]{1,0:T(8,128)}, f32[64,1024]{1,0:T(8,128)}, u32[]{:S(2)}, u32[]{:S(2)}) collective-permute-start(f32[64,1024]{1,0:T(8,128)} %get-tuple-element.75), channel_id=1, source_target_pairs={{0,1},{1,0},{2,3},{3,2},{4,5},{5,4},{6,7},{7,6},{8,9},{9,8},{10,11... | collective-permute-start | bytes 786440 | tf_op jit(solution)/shard_map/ppermute | solution.py:23
  200.6 7.9 %shard_map.108 = (bf16[512,2048]{1,0:T(8,128)(2,1)}, f32[2048,512]{1,0:T(8,128)}, f32[2048,512]{1,0:T(8,128)}, f32[1,16,128,128]{3,2,1,0:T(8,128)}, f32[16,8,512]{2,1,0:T(8,128)S(1)}) custom-call(s32[2]{0:T(128)S(1)} %copy-done.19, bf16[2048,512]{1,0:T(8,128)(2,1)S(1)} %copy-done.7, ...), custom_call_target="tpu_custom_call", output_to_operand_aliasing={{0}: (9, {}), {1}: (10, {}), {2}: (11, {}), {3}: (12, {}), ... | custom-call | flops 1879048192 | bytes 10485760 | tf_op jit(solution)/shard_map/pallas_call | solution.py:420
  208.6 4.8 %shard_map.109 = (bf16[512,2048]{1,0:T(8,128)(2,1)}, f32[2048,512]{1,0:T(8,128)}, f32[2048,512]{1,0:T(8,128)}, f32[1,16,128,128]{3,2,1,0:T(8,128)}, f32[16,8,512]{2,1,0:T(8,128)S(1)}) custom-call(s32[2]{0:T(128)S(1)} %copy-done.19, bf16[2048,512]{1,0:T(8,128)(2,1)S(1)} %copy-done.7, ...), custom_call_target="tpu_custom_call", output_to_operand_aliasing={{0}: (9, {}), {1}: (10, {}), {2}: (11, {}), {3}: (12, {}), ... | custom-call | flops 939524096 | bytes 5242880 | tf_op jit(solution)/shard_map/pallas_call | solution.py:420
  217.0 8.9 %shard_map.111 = (bf16[512,2048]{1,0:T(8,128)(2,1)}, bf16[512,2048]{1,0:T(8,128)(2,1)}) custom-call(s32[2]{0:T(128)} %pad_add_fusion.bits_ref, bf16[512,2048]{1,0:T(8,128)(2,1)} %bitcast.106, bf16[512,2048]{1,0:T(8,128)(2,1)} %bitcast.113, f32[2048,512]{1,0:T(8,128)} %get-tuple-element.55.gk_ref, f32[2048,512]{1,0:T(8,128)} %get-tuple-element.56.gv_ref, ...), custom_call_target="tpu_custom_call" | custom-call | flops 536870912 | bytes 16777216 | tf_op jit(solution)/shard_map/pallas_call | solution.py:438
  (93 shorter events, 39.2 us)
Async XLA Ops:
  0.6 24.9 %copy-start.23 = (f32[1,512,128]{2,1,0:T(8,128)S(1)}, f32[1,512,128]{2,1,0:T(8,128)}, u32[]{:S(2)}) copy-start(f32[1,512,128]{2,1,0:T(8,128)} %param.9) | copy-start | bytes 786436
  5.5 18.3 %copy-start.2 = (bf16[1,512,2048]{2,1,0:T(8,128)(2,1)S(1)}, bf16[1,512,2048]{2,1,0:T(8,128)(2,1)}, u32[]{:S(2)}) copy-start(bf16[1,512,2048]{2,1,0:T(8,128)(2,1)} %param.11) | copy-start | bytes 6291460
  5.5 13.9 %collective-permute-start.7 = (bf16[16,128,128]{2,1,0:T(8,128)(2,1)}, bf16[16,128,128]{2,1,0:T(8,128)(2,1)S(1)}, u32[]{:S(2)}, u32[]{:S(2)}) collective-permute-start(bf16[16,128,128]{2,1,0:T(8,128)(2,1)} %get-tuple-element.42), channel_id=1, source_target_pairs={{0,8},{8,0},{16,24},{24,16},{1,9},{9,1},{17,25},{25,17},{2,10},{10... | collective-permute-start | bytes 1572872 | tf_op jit(solution)/shard_map/ppermute | solution.py:23
  21.6 25.3 %collective-permute-start.8 = (bf16[16,128,128]{2,1,0:T(8,128)(2,1)}, bf16[16,128,128]{2,1,0:T(8,128)(2,1)S(1)}, u32[]{:S(2)}, u32[]{:S(2)}) collective-permute-start(bf16[16,128,128]{2,1,0:T(8,128)(2,1)} %add_convert_fusion.1), channel_id=1, source_target_pairs={{0,16},{8,24},{16,0},{24,8},{1,17},{9,25},{17,1},{25,9},{2,18},{10... | collective-permute-start | bytes 1572872 | tf_op jit(solution)/shard_map/ppermute | solution.py:23
  23.8 32.3 %collective-permute-start.13 = (bf16[512,2048]{1,0:T(8,128)(2,1)S(1)}, bf16[512,2048]{1,0:T(8,128)(2,1)}, u32[]{:S(2)}, u32[]{:S(2)}) collective-permute-start(bf16[512,2048]{1,0:T(8,128)(2,1)S(1)} %bitcast.117), channel_id=1, source_target_pairs={{0,1},{1,0},{2,3},{3,2},{4,5},{5,4},{6,7},{7,6},{8,9},{9,8},{10,11... | collective-permute-start | bytes 6291464 | tf_op jit(solution)/shard_map/ppermute | solution.py:23
  46.8 7.8 %copy-start.11 = (bf16[16,128,128]{2,1,0:T(8,128)(2,1)}, bf16[16,128,128]{2,1,0:T(8,128)(2,1)S(1)}, u32[]{:S(2)}) copy-start(bf16[16,128,128]{2,1,0:T(8,128)(2,1)S(1)} %collective-permute-done.8.refs_1_) | copy-start | bytes 1572868
  54.6 5.5 %collective-permute-start.12 = (bf16[2048,512]{1,0:T(8,128)(2,1)}, bf16[2048,512]{1,0:T(8,128)(2,1)}, u32[]{:S(2)}, u32[]{:S(2)}) collective-permute-start(bf16[2048,512]{1,0:T(8,128)(2,1)} %shard_map.112.attn_ref), channel_id=1, source_target_pairs={{0,1},{1,0},{2,3},{3,2},{4,5},{5,4},{6,7},{7,6},{8,9},{9,8},{10,11... | collective-permute-start | bytes 6291464 | tf_op jit(solution)/shard_map/ppermute | solution.py:23
  65.9 24.7 %collective-permute-start.14 = (bf16[1024,512]{1,0:T(8,128)(2,1)}, bf16[1024,512]{1,0:T(8,128)(2,1)}, u32[]{:S(2)}, u32[]{:S(2)}) collective-permute-start(bf16[1024,512]{1,0:T(8,128)(2,1)} %get-tuple-element.66), channel_id=1, source_target_pairs={{0,2},{1,3},{2,0},{3,1},{4,6},{5,7},{6,4},{7,5},{8,10},{9,11},{10,... | collective-permute-start | bytes 3145736 | tf_op jit(solution)/shard_map/ppermute | solution.py:23
  67.0 32.4 %collective-permute-start.16 = (bf16[1024,512]{1,0:T(8,128)(2,1)}, bf16[1024,512]{1,0:T(8,128)(2,1)}, u32[]{:S(2)}, u32[]{:S(2)}) collective-permute-start(bf16[1024,512]{1,0:T(8,128)(2,1)} %get-tuple-element.68), channel_id=1, source_target_pairs={{0,4},{1,5},{2,6},{3,7},{4,0},{5,1},{6,2},{7,3},{8,12},{9,13},{10,... | collective-permute-start | bytes 3145736 | tf_op jit(solution)/shard_map/ppermute | solution.py:23
  68.3 45.6 %collective-permute-start.3 = (bf16[256,2048]{1,0:T(8,128)(2,1)}, bf16[256,2048]{1,0:T(8,128)(2,1)}, u32[]{:S(2)}, u32[]{:S(2)}) collective-permute-start(bf16[256,2048]{1,0:T(8,128)(2,1)} %refs_0_.1), channel_id=1, source_target_pairs={{0,4},{1,5},{2,6},{3,7},{4,0},{5,1},{6,2},{7,3},{8,12},{9,13},{10,... | collective-permute-start | bytes 3145736 | tf_op jit(solution)/shard_map/ppermute | solution.py:23
  68.5 45.9 %collective-permute-start.2 = (bf16[256,2048]{1,0:T(8,128)(2,1)}, bf16[256,2048]{1,0:T(8,128)(2,1)}, u32[]{:S(2)}, u32[]{:S(2)}) collective-permute-start(bf16[256,2048]{1,0:T(8,128)(2,1)} %refs_0_.1), channel_id=1, source_target_pairs={{0,2},{1,3},{2,0},{3,1},{4,6},{5,7},{6,4},{7,5},{8,10},{9,11},{10,... | collective-permute-start | bytes 3145736 | tf_op jit(solution)/shard_map/ppermute | solution.py:23
  68.9 70.6 %collective-permute-start = (bf16[256,2048]{1,0:T(8,128)(2,1)}, bf16[256,2048]{1,0:T(8,128)(2,1)}, u32[]{:S(2)}, u32[]{:S(2)}) collective-permute-start(bf16[256,2048]{1,0:T(8,128)(2,1)} %refs_0_.1), channel_id=1, source_target_pairs={{0,6},{1,7},{2,4},{3,5},{4,2},{5,3},{6,0},{7,1},{8,14},{9,15},{10,... | collective-permute-start | bytes 3145736 | tf_op jit(solution)/shard_map/ppermute | solution.py:23
  90.6 49.0 %collective-permute-start.6 = (bf16[256,2048]{1,0:T(8,128)(2,1)}, bf16[256,2048]{1,0:T(8,128)(2,1)}, u32[]{:S(2)}, u32[]{:S(2)}) collective-permute-start(bf16[256,2048]{1,0:T(8,128)(2,1)} %refs_0_.1), channel_id=1, source_target_pairs={{0,1},{1,0},{2,3},{3,2},{4,5},{5,4},{6,7},{7,6},{8,9},{9,8},{10,11... | collective-permute-start | bytes 3145736 | tf_op jit(solution)/shard_map/ppermute | solution.py:23
  97.8 4.8 %copy-start.13 = (f32[1024,512]{1,0:T(8,128)}, f32[1024,512]{1,0:T(8,128)S(1)}, u32[]{:S(2)}) copy-start(f32[1024,512]{1,0:T(8,128)S(1)} %get-tuple-element.67) | copy-start | bytes 6291460
  99.4 48.2 %collective-permute-start.15 = (bf16[4,128,512]{2,1,0:T(8,128)(2,1)S(1)}, bf16[4,128,512]{2,1,0:T(8,128)(2,1)}, u32[]{:S(2)}, u32[]{:S(2)}) collective-permute-start(bf16[4,128,512]{2,1,0:T(8,128)(2,1)S(1)} %fusion.9), channel_id=1, source_target_pairs={{0,4},{1,5},{2,6},{3,7},{4,0},{5,1},{6,2},{7,3},{8,12},{9,13},{10,... | collective-permute-start | bytes 1572872 | tf_op jit(solution)/shard_map/ppermute | solution.py:23
  113.9 35.2 %collective-permute-start.17 = (bf16[4,128,512]{2,1,0:T(8,128)(2,1)}, bf16[4,128,512]{2,1,0:T(8,128)(2,1)}, u32[]{:S(2)}, u32[]{:S(2)}) collective-permute-start(bf16[4,128,512]{2,1,0:T(8,128)(2,1)} %fusion.10), channel_id=1, source_target_pairs={{0,2},{1,3},{2,0},{3,1},{4,6},{5,7},{6,4},{7,5},{8,10},{9,11},{10,... | collective-permute-start | bytes 1572872 | tf_op jit(solution)/shard_map/ppermute | solution.py:23
  114.4 33.2 %copy-start.16 = (f32[1024,512]{1,0:T(8,128)S(1)}, f32[1024,512]{1,0:T(8,128)}, u32[]{:S(2)}) copy-start(f32[1024,512]{1,0:T(8,128)} %copy-done.15) | copy-start | bytes 6291460
  114.4 37.8 %collective-permute-start.5 = (bf16[256,2048]{1,0:T(8,128)(2,1)}, bf16[256,2048]{1,0:T(8,128)(2,1)S(1)}, u32[]{:S(2)}, u32[]{:S(2)}) collective-permute-start(bf16[256,2048]{1,0:T(8,128)(2,1)} %collective-permute-done.3.refs_1_), channel_id=1, source_target_pairs={{0,1},{1,0},{2,3},{3,2},{4,5},{5,4},{6,7},{7,6},{8,9},{9,8},{10,11... | collective-permute-start | bytes 3145736 | tf_op jit(solution)/shard_map/ppermute | solution.py:23
  139.5 12.7 %collective-permute-start.4 = (bf16[256,2048]{1,0:T(8,128)(2,1)}, bf16[256,2048]{1,0:T(8,128)(2,1)S(1)}, u32[]{:S(2)}, u32[]{:S(2)}) collective-permute-start(bf16[256,2048]{1,0:T(8,128)(2,1)} %collective-permute-done.2.refs_0_), channel_id=1, source_target_pairs={{0,1},{1,0},{2,3},{3,2},{4,5},{5,4},{6,7},{7,6},{8,9},{9,8},{10,11... | collective-permute-start | bytes 3145736 | tf_op jit(solution)/shard_map/ppermute | solution.py:23
  139.6 18.5 %collective-permute-start.1 = (bf16[256,2048]{1,0:T(8,128)(2,1)}, bf16[256,2048]{1,0:T(8,128)(2,1)S(1)}, u32[]{:S(2)}, u32[]{:S(2)}) collective-permute-start(bf16[256,2048]{1,0:T(8,128)(2,1)} %collective-permute-done.refs_0_), channel_id=1, source_target_pairs={{0,1},{1,0},{2,3},{3,2},{4,5},{5,4},{6,7},{7,6},{8,9},{9,8},{10,11... | collective-permute-start | bytes 3145736 | tf_op jit(solution)/shard_map/ppermute | solution.py:23
  151.7 28.1 %collective-permute-start.18 = (bf16[2,128,1024]{2,1,0:T(8,128)(2,1)}, bf16[2,128,1024]{2,1,0:T(8,128)(2,1)}, u32[]{:S(2)}, u32[]{:S(2)}) collective-permute-start(bf16[2,128,1024]{2,1,0:T(8,128)(2,1)} %fusion.11), channel_id=1, source_target_pairs={{0,8},{8,0},{16,24},{24,16},{1,9},{9,1},{17,25},{25,17},{2,10},{10... | collective-permute-start | bytes 1572872 | tf_op jit(solution)/shard_map/ppermute | solution.py:23
  164.0 5.2 %copy-start = (bf16[1,512,2048]{2,1,0:T(8,128)(2,1)S(1)}, bf16[1,512,2048]{2,1,0:T(8,128)(2,1)}, u32[]{:S(2)}) copy-start(bf16[1,512,2048]{2,1,0:T(8,128)(2,1)} %param.7) | copy-start | bytes 6291460
  164.0 5.2 %copy-start.9 = (bf16[1,16,128,128]{3,2,1,0:T(8,128)(2,1)S(1)}, bf16[1,16,128,128]{3,2,1,0:T(8,128)(2,1)}, u32[]{:S(2)}) copy-start(bf16[1,16,128,128]{3,2,1,0:T(8,128)(2,1)} %get-tuple-element.37.block_ref) | copy-start | bytes 1572868
  164.0 5.2 %copy-start.10 = (f32[1,512,128]{1,2,0:T(8,128)S(1)}, f32[1,512,128]{1,2,0:T(8,128)}, u32[]{:S(2)}) copy-start(f32[1,512,128]{1,2,0:T(8,128)} %copy.34) | copy-start | bytes 786436
  164.0 5.2 %copy-start.19 = (s32[2]{0:T(128)S(1)}, s32[2]{0:T(128)}, u32[]{:S(2)}) copy-start(s32[2]{0:T(128)} %pad_add_fusion.bits_ref) | copy-start | bytes 28
  167.7 16.2 %collective-permute-start.9 = (bf16[16,128,128]{2,1,0:T(8,128)(2,1)}, bf16[16,128,128]{2,1,0:T(8,128)(2,1)}, u32[]{:S(2)}, u32[]{:S(2)}) collective-permute-start(bf16[16,128,128]{2,1,0:T(8,128)(2,1)} %get-tuple-element.59), channel_id=1, source_target_pairs={{8,0},{24,16},{9,1},{25,17},{10,2},{26,18},{11,3},{27,19},{12,4},{... | collective-permute-start | bytes 1572872 | tf_op jit(solution)/shard_map/ppermute | solution.py:391
  175.0 8.8 %copy-start.18 = (f32[16,128,128]{2,1,0:T(8,128)S(1)}, f32[16,128,128]{2,1,0:T(8,128)}, u32[]{:S(2)}) copy-start(f32[16,128,128]{2,1,0:T(8,128)} %copy-done.17) | copy-start | bytes 3145732
  180.8 12.7 %collective-permute-start.19 = (bf16[128,1024]{1,0:T(8,128)(2,1)S(1)}, bf16[128,1024]{1,0:T(8,128)(2,1)S(1)}, u32[]{:S(2)}, u32[]{:S(2)}) collective-permute-start(bf16[128,1024]{1,0:T(8,128)(2,1)S(1)} %fusion.13), channel_id=1, source_target_pairs={{0,16},{8,24},{16,0},{24,8},{1,17},{9,25},{17,1},{25,9},{2,18},{10... | collective-permute-start | bytes 786440 | tf_op jit(solution)/shard_map/ppermute | solution.py:23
  185.8 29.4 %collective-permute-start.11 = (bf16[16,128,128]{2,1,0:T(8,128)(2,1)}, bf16[16,128,128]{2,1,0:T(8,128)(2,1)}, u32[]{:S(2)}, u32[]{:S(2)}) collective-permute-start(bf16[16,128,128]{2,1,0:T(8,128)(2,1)} %add_convert_fusion), channel_id=1, source_target_pairs={{16,8},{24,16},{17,9},{25,17},{18,10},{26,18},{19,11},{27,19},{20,... | collective-permute-start | bytes 1572872 | tf_op jit(solution)/shard_map/ppermute | solution.py:393
  187.4 29.6 %collective-permute-start.10 = (bf16[16,128,128]{2,1,0:T(8,128)(2,1)}, bf16[16,128,128]{2,1,0:T(8,128)(2,1)}, u32[]{:S(2)}, u32[]{:S(2)}) collective-permute-start(bf16[16,128,128]{2,1,0:T(8,128)(2,1)} %add_convert_fusion), channel_id=1, source_target_pairs={{16,0},{17,1},{18,2},{19,3},{20,4},{21,5},{22,6},{23,7}} | collective-permute-start | bytes 1572872 | tf_op jit(solution)/shard_map/ppermute | solution.py:393
  195.4 30.5 %collective-permute-start.20 = (f32[64,1024]{1,0:T(8,128)}, f32[64,1024]{1,0:T(8,128)}, u32[]{:S(2)}, u32[]{:S(2)}) collective-permute-start(f32[64,1024]{1,0:T(8,128)} %get-tuple-element.75), channel_id=1, source_target_pairs={{0,1},{1,0},{2,3},{3,2},{4,5},{5,4},{6,7},{7,6},{8,9},{9,8},{10,11... | collective-permute-start | bytes 786440 | tf_op jit(solution)/shard_map/ppermute | solution.py:23
  217.0 8.9 %copy-start.22 = (f32[64,1024]{1,0:T(8,128)S(1)}, f32[64,1024]{1,0:T(8,128)}, u32[]{:S(2)}) copy-start(f32[64,1024]{1,0:T(8,128)} %get-tuple-element.74) | copy-start | bytes 786436
  (13 other events, 33.2 us)

commit v3 on v2

--- a/solution.py
+++ b/solution.py
@@ -70,17 +70,15 @@
     return blocks
 
 
-def states_body(k_ref, v_ref, wide_ref, half_ref, block_ref):
+def states_body(k_ref, v_ref, half_ref, block_ref):
     seg_len = k_ref.shape[0]
-    for i in range(wide_ref.shape[0]):
+    for i in range(half_ref.shape[0]):
         cols = slice(i * HD, (i + 1) * HD)
         tiles = [
             mm(k_ref[start : start + TILE, cols], v_ref[start : start + TILE, cols], 0, 0)
             for start in range(0, seg_len, TILE)
         ]
-        state = sum(tiles[1:], tiles[0])
-        wide_ref[i] = state
-        half_ref[i] = state.astype(BF)
+        half_ref[i] = sum(tiles[1:], tiles[0]).astype(BF)
         for j, (_, _, col, size) in enumerate(far_blocks(seg_len)):
             part = tiles[col // TILE : (col + size) // TILE]
             block_ref[j, i] = sum(part[1:], part[0]).astype(BF)
@@ -285,20 +283,19 @@
     whole_gain = pl.BlockSpec((LEVELS * H, seg_len), lambda h, *_: (0, 0))
     gain = gain.T
 
-    state_wide, state_half, blocks = call(
+    state_half, blocks = call(
         states_body, head_flops, 2 * tok_bytes, EARLY,
-        out_shape=(sds(mats, F32), sds(mats, BF), sds((n_blocks,) + mats, BF)),
+        out_shape=(sds(mats, BF), sds((n_blocks,) + mats, BF)),
         grid=(H // 4,), in_specs=[cols(4), cols(4)],
-        out_specs=(mat(4), mat(4), stack(n_blocks, 4)),
+        out_specs=(mat(4), stack(n_blocks, 4)),
     )(k, v)
     fars = []
-    running_wide, running = state_wide, state_half
+    running = state_half
     for b in range(n_bits):
         received = swapped(running, "seq", 1 << b)
         fars.append(received)
         if b + 1 < n_bits:
-            running_wide = running_wide + received.astype(F32)
-            running = running_wide.astype(BF)
+            running = (running.astype(F32) + received.astype(F32)).astype(BF)
 
     if fast:
         pieces = {0: out_weight}
@@ -310,7 +307,7 @@
         pieces[5] = swapped(pieces[4], "batch", 1)
         pieces[6] = swapped(out_weight, "batch", 6)
         pieces[7] = swapped(pieces[6], "batch", 1)
-        stages = [[(pieces[m], batch_index ^ m) for m in group] for group in ((0, 1), (2, 4, 3, 5), (6, 7))]
+        stages = [[(pieces[m], batch_index ^ m) for m in group] for group in ((0, 1), (2, 4), (3, 5), (6, 7))]
         g = None
         for stage in stages:
             count, piece_rows = len(stage), stage[0][0].shape[0]
@@ -410,7 +407,7 @@
         gates = tuple((b,) for b in range(n_bits))
 
     done = []
-    bounds = (0, H // 8, 3 * H // 8, H // 2)
+    bounds = (0, H // 16, 5 * H // 16, H // 2)
     for first, last in zip(bounds, bounds[1:]):
         two = pl.BlockSpec((seg_len, 2 * HD), lambda h, *_, first=first: (0, h + first))
         two_turned = pl.BlockSpec((2 * HD, seg_len), lambda h, *_, first=first: (h + first, 0))

time: 231 us -> 227 us (0.983)
  starting transfers between devices: 54.7 us -> 52 us
    ppermute x18, starting transfers between devices: 50.4 us -> 47.8 us  [swapped(): lax.ppermute(value, axis, [(source, source ^ mask) for source in range(la...]
    pallas_call x3 -> x4, Pallas kernels: 14.5 us -> 15.4 us  [step(): call(functools.partial(attn_grad_body, count), 2 * seg_len * width * piec...]
    unnamed x50 -> x42, local copies, waits for them, and re-layouts: 14.7 us -> 14.7 us
  transfers between devices with their start and end apart: 21 -> 21, of which waited for: 8 -> 8; matrix products, arithmetic and copies ran while one was open for 7% -> 7% of each run, Pallas kernels for 29% -> 30%
where the time goes in v3:
time: 227 us; the launch traced here: 224 us
  Pallas kernels  76.8 us (34%)
  waiting for transfers between devices  62.9 us (28%)
  starting transfers between devices  52 us (23%)
  local copies, waits for them, and re-layouts  17.5 us (8%)
  other arithmetic  14.2 us (6%)
    ppermute x18, waiting for transfers between devices, swapped(): lax.ppermute(value, axis, [(source, source ^ mask) for source in range(la...  60.5 us
    ppermute x18, starting transfers between devices, swapped(): lax.ppermute(value, axis, [(source, source ^ mask) for source in range(la...  47.8 us
    pallas_call x3, Pallas kernels, step(): call(functools.partial(main_body, n_bits, 2, first * 2, len(done)), (5 *...  17.5 us
    pallas_call x4, Pallas kernels, step(): call(functools.partial(attn_grad_body, count), 2 * seg_len * width * piec...  15.4 us
    unnamed x42, local copies, waits for them, and re-layouts  14.7 us
    pallas_call x2, Pallas kernels, step(): call(functools.partial(intra_body, n_bits, 4, first * 4), 2 * seg_len * T...  13.6 us
    pallas_call x2, Pallas kernels, products(): call(functools.partial(weight_body, picks), 4 * seg_len * width * quarter...  10.8 us
    pallas_call x1, Pallas kernels, step(): call(functools.partial(final_body, 4, gates), 2 * head_flops, 8 * tok_byt...  8.9 us
  transfers between devices with their start and end apart: 21, of which 8 were waited for; matrix products, arithmetic and copies ran while one was open for 7% of the time, Pallas kernels for 30%

profile of v3, /device:TPU:1, one launch (start us, length us, event | category | flops | bytes accessed | tf_op | source)
XLA Modules:
  0.0 224.2 jit_solution(6746734117862588218)
XLA Ops:
  0.7 4.7 %shard_map.101 = (bf16[16,128,128]{2,1,0:T(8,128)(2,1)}, bf16[1,16,128,128]{3,2,1,0:T(8,128)(2,1)}) custom-call(bf16[512,2048]{1,0:T(8,128)(2,1)} %bitcast.112, bf16[512,2048]{1,0:T(8,128)(2,1)} %bitcast.119), custom_call_target="tpu_custom_call" | custom-call | flops 268435456 | bytes 4194304 | tf_op jit(solution)/shard_map/pallas_call | solution.py:286
  5.4 2.1 collective-permute-start.7
  7.5 11.8 %collective-permute-done.7.refs_0_ = bf16[16,128,128]{2,1,0:T(8,128)(2,1)S(1)} collective-permute-done((bf16[16,128,128]{2,1,0:T(8,128)(2,1)}, bf16[16,128,128]{2,1,0:T(8,128)(2,1)S(1)}, u32[]{:S(2)}, u32[]{:S(2)}) %collective-permute-start.7) | collective-permute-done | bytes 524320 | tf_op jit(solution)/shard_map/ppermute | solution.py:23
  21.3 2.2 collective-permute-start.8
  26.8 6.9 %shard_map.102 = (f32[2048,512]{1,0:T(8,128)}, bf16[4096,512]{1,0:T(8,128)(2,1)}, bf16[2048,512]{1,0:T(8,128)(2,1)}) custom-call(s32[2]{0:T(128)} %pad_add_fusion.bits_ref, bf16[512,2048]{1,0:T(8,128)(2,1)} %bitcast.136, bf16[512,2048]{1,0:T(8,128)(2,1)} %bitcast.113, bf16[512,2048]{1,0:T(8,128)(2,1)} %bitcast.120, f32[128,512]{1,0:T(8,128)} %bitcast.126, ...), custom_call_target="tpu_custom_call" | custom-call | flops 536870912 | bytes 10485760 | tf_op jit(solution)/shard_map/pallas_call | solution.py:341
  33.7 6.7 %shard_map.103 = (f32[2048,512]{1,0:T(8,128)}, bf16[4096,512]{1,0:T(8,128)(2,1)}, bf16[2048,512]{1,0:T(8,128)(2,1)}) custom-call(s32[2]{0:T(128)} %pad_add_fusion.bits_ref, bf16[512,2048]{1,0:T(8,128)(2,1)} %bitcast.137, bf16[512,2048]{1,0:T(8,128)(2,1)} %bitcast.114, ...), custom_call_target="tpu_custom_call", output_to_operand_aliasing={{0}: (6, {}), {1}: (7, {}), {2}: (8, {})} | custom-call | flops 536870912 | bytes 10485760 | tf_op jit(solution)/shard_map/pallas_call | solution.py:341
  40.5 6.1 %collective-permute-done.8.refs_1_ = bf16[16,128,128]{2,1,0:T(8,128)(2,1)S(1)} collective-permute-done((bf16[16,128,128]{2,1,0:T(8,128)(2,1)}, bf16[16,128,128]{2,1,0:T(8,128)(2,1)S(1)}, u32[]{:S(2)}, u32[]{:S(2)}) %collective-permute-start.8) | collective-permute-done | bytes 524320 | tf_op jit(solution)/shard_map/ppermute | solution.py:23
  46.6 2.4 %copy-done.5 = bf16[4096,512]{1,0:T(8,128)(2,1)S(1)} copy-done((bf16[4096,512]{1,0:T(8,128)(2,1)S(1)}, bf16[4096,512]{1,0:T(8,128)(2,1)}, u32[]{:S(2)}) %copy-start.5) | copy-done | bytes 4194328
  49.0 2.2 copy-done.8
  51.2 3.2 %shard_map.113.attn_ref = bf16[2048,512]{1,0:T(8,128)(2,1)} custom-call(s32[2]{0:T(128)S(1)} %pad_add_fusion.5.at_ref, bf16[4096,512]{1,0:T(8,128)(2,1)S(1)} %copy-done.5, f32[2048,512]{1,0:T(8,128)S(1)} %copy-done.8, bf16[16,128,128]{2,1,0:T(8,128)(2,1)S(1)} %collective-permute-done.7.refs_0_, bf16[16,128,128]{2,1,0:T(8,128)(2,1)S(1)} %collective-permute-done.8.refs_1_), custom_call_target="tpu_custom_call" | custom-call | flops 536870912 | bytes 10485760 | tf_op jit(solution)/shard_map/pallas_call | solution.py:358
  55.7 4.1 %collective-permute-done.12.attn2_ref = bf16[2048,512]{1,0:T(8,128)(2,1)} collective-permute-done((bf16[2048,512]{1,0:T(8,128)(2,1)}, bf16[2048,512]{1,0:T(8,128)(2,1)}, u32[]{:S(2)}, u32[]{:S(2)}) %collective-permute-start.12) | collective-permute-done | bytes 2097184 | tf_op jit(solution)/shard_map/ppermute | solution.py:23
  59.9 5.8 %shard_map.115 = (bf16[1024,512]{1,0:T(8,128)(2,1)}, bf16[1024,512]{1,0:T(8,128)(2,1)}) custom-call(s32[1]{0:T(128)} %bitcast.24.core_ref, bf16[2048,512]{1,0:T(8,128)(2,1)} %shard_map.113.attn_ref, bf16[2048,512]{1,0:T(8,128)(2,1)} %collective-permute-done.12.attn2_ref, bf16[512,2048]{1,0:T(8,128)(2,1)S(1)} %bitcast.104, ...), custom_call_target="tpu_custom_call" | custom-call | flops 2147483648 | bytes 8388608 | tf_op jit(solution)/shard_map/pallas_call | solution.py:459
  68.6 2.1 collective-permute-start
  70.7 19.6 %collective-permute-done.14 = bf16[1024,512]{1,0:T(8,128)(2,1)} collective-permute-done((bf16[1024,512]{1,0:T(8,128)(2,1)}, bf16[1024,512]{1,0:T(8,128)(2,1)}, u32[]{:S(2)}, u32[]{:S(2)}) %collective-permute-start.14) | collective-permute-done | bytes 1048608 | tf_op jit(solution)/shard_map/ppermute | solution.py:23
  90.3 2.1 collective-permute-start.6
  92.5 5.0 %shard_map.114 = (f32[1024,512]{1,0:T(8,128)S(1)}, f32[1024,512]{1,0:T(8,128)S(1)}) custom-call(s32[1]{0:T(128)} %bitcast.24.core_ref, bf16[2048,512]{1,0:T(8,128)(2,1)} %shard_map.113.attn_ref, bf16[2048,512]{1,0:T(8,128)(2,1)} %collective-permute-done.12.attn2_ref, bf16[512,2048]{1,0:T(8,128)(2,1)S(1)} %bitcast.106, ...), custom_call_target="tpu_custom_call" | custom-call | flops 2147483648 | bytes 8388608 | tf_op jit(solution)/shard_map/pallas_call | solution.py:459
  101.3 12.4 %collective-permute-done.4.refs_1_ = bf16[256,2048]{1,0:T(8,128)(2,1)} collective-permute-done((bf16[256,2048]{1,0:T(8,128)(2,1)}, bf16[256,2048]{1,0:T(8,128)(2,1)}, u32[]{:S(2)}, u32[]{:S(2)}) %collective-permute-start.4) | collective-permute-done | bytes 1048608 | tf_op jit(solution)/shard_map/ppermute | solution.py:23
  114.1 25.0 %collective-permute-start.5 = (bf16[256,2048]{1,0:T(8,128)(2,1)}, bf16[256,2048]{1,0:T(8,128)(2,1)S(1)}, u32[]{:S(2)}, u32[]{:S(2)}) collective-permute-start(bf16[256,2048]{1,0:T(8,128)(2,1)} %collective-permute-done.4.refs_1_), channel_id=1, source_target_pairs={{0,1},{1,0},{2,3},{3,2},{4,5},{5,4},{6,7},{7,6},{8,9},{9,8},{10,11... | collective-permute-start | bytes 3145736 | tf_op jit(solution)/shard_map/ppermute | solution.py:23
  139.6 4.0 %shard_map.104.refs_2_ = bf16[2048,512]{1,0:T(8,128)(2,1)} custom-call(s32[2]{0:T(128)S(1)} %pad_add_fusion.4.at_ref, bf16[512,2048]{1,0:T(8,128)(2,1)S(1)} %bitcast.108, bf16[256,2048]{1,0:T(8,128)(2,1)} %refs_0_.1, bf16[256,2048]{1,0:T(8,128)(2,1)S(1)} %collective-permute-done.6.refs_1_), custom_call_target="tpu_custom_call" | custom-call | flops 1073741824 | bytes 4718592 | tf_op jit(solution)/shard_map/pallas_call | solution.py:317
  143.6 4.3 %shard_map.105.refs_2_ = bf16[2048,512]{1,0:T(8,128)(2,1)} custom-call(s32[2]{0:T(128)S(1)} %pad_add_fusion.3.at_ref, bf16[512,2048]{1,0:T(8,128)(2,1)S(1)} %bitcast.109, bf16[256,2048]{1,0:T(8,128)(2,1)} %collective-permute-done.2.refs_0_, bf16[256,2048]{1,0:T(8,128)(2,1)} %collective-permute-done.4.refs_1_, ...), custom_call_target="tpu_custom_call", output_to_operand_aliasing={{}: (4, {})} | custom-call | flops 1073741824 | bytes 4718592 | tf_op jit(solution)/shard_map/pallas_call | solution.py:317
  152.4 2.8 %shard_map.106.refs_2_ = bf16[2048,512]{1,0:T(8,128)(2,1)} custom-call(s32[2]{0:T(128)S(1)} %pad_add_fusion.2.at_ref, bf16[512,2048]{1,0:T(8,128)(2,1)S(1)} %bitcast.110, bf16[256,2048]{1,0:T(8,128)(2,1)S(1)} %collective-permute-done.3.refs_0_, bf16[256,2048]{1,0:T(8,128)(2,1)S(1)} %collective-permute-done.5.refs_1_, ...), custom_call_target="tpu_custom_call", output_to_operand_aliasing={{}: (4, {})} | custom-call | flops 1073741824 | bytes 4718592 | tf_op jit(solution)/shard_map/pallas_call | solution.py:317
  155.2 4.3 %shard_map.107.g_ref = bf16[2048,512]{1,0:T(8,128)(2,1)} custom-call(s32[2]{0:T(128)S(1)} %pad_add_fusion.1.at_ref, bf16[512,2048]{1,0:T(8,128)(2,1)S(1)} %bitcast.111, bf16[256,2048]{1,0:T(8,128)(2,1)} %collective-permute-done.refs_0_, bf16[256,2048]{1,0:T(8,128)(2,1)S(1)} %collective-permute-done.1.refs_1_, ...), custom_call_target="tpu_custom_call", output_to_operand_aliasing={{}: (4, {})} | custom-call | flops 1073741824 | bytes 4718592 | tf_op jit(solution)/shard_map/pallas_call | solution.py:317
  161.1 2.7 %shard_map.111 = (bf16[16,128,128]{2,1,0:T(8,128)(2,1)}, f32[16,128,128]{2,1,0:T(8,128)S(1)}) custom-call(s32[1]{0:T(128)} %bitcast.18.at_ref, bf16[4096,512]{1,0:T(8,128)(2,1)S(1)} %copy-done.6, bf16[2048,512]{1,0:T(8,128)(2,1)S(1)} %copy-done.1), custom_call_target="tpu_custom_call" | custom-call | flops 536870912 | bytes 8388608 | tf_op jit(solution)/shard_map/pallas_call | solution.py:380
  172.1 3.1 %shard_map.108 = (bf16[512,2048]{1,0:T(8,128)(2,1)}, f32[2048,512]{1,0:T(8,128)}, f32[2048,512]{1,0:T(8,128)}, f32[1,16,128,128]{3,2,1,0:T(8,128)}, f32[16,8,512]{2,1,0:T(8,128)S(1)}) custom-call(s32[2]{0:T(128)S(1)} %copy-done.15, bf16[2048,512]{1,0:T(8,128)(2,1)S(1)} %copy-done.7, bf16[512,2048]{1,0:T(8,128)(2,1)S(1)} %bitcast.116, ...), custom_call_target="tpu_custom_call" | custom-call | flops 469762048 | bytes 2621440 | tf_op jit(solution)/shard_map/pallas_call | solution.py:417
  176.2 3.1 %collective-permute-start.19 = (bf16[128,1024]{1,0:T(8,128)(2,1)S(1)}, bf16[128,1024]{1,0:T(8,128)(2,1)S(1)}, u32[]{:S(2)}, u32[]{:S(2)}) collective-permute-start(bf16[128,1024]{1,0:T(8,128)(2,1)S(1)} %fusion.13), channel_id=1, source_target_pairs={{0,16},{8,24},{16,0},{24,8},{1,17},{9,25},{17,1},{25,9},{2,18},{10... | collective-permute-start | bytes 786440 | tf_op jit(solution)/shard_map/ppermute | solution.py:23
  179.6 2.0 add_convert_fusion
  184.4 6.4 %collective-permute-done.19 = bf16[128,1024]{1,0:T(8,128)(2,1)S(1)} collective-permute-done((bf16[128,1024]{1,0:T(8,128)(2,1)S(1)}, bf16[128,1024]{1,0:T(8,128)(2,1)S(1)}, u32[]{:S(2)}, u32[]{:S(2)}) %collective-permute-start.19) | collective-permute-done | bytes 262176 | tf_op jit(solution)/shard_map/ppermute | solution.py:23
  192.8 2.3 %collective-permute-start.20 = (f32[64,1024]{1,0:T(8,128)}, f32[64,1024]{1,0:T(8,128)}, u32[]{:S(2)}, u32[]{:S(2)}) collective-permute-start(f32[64,1024]{1,0:T(8,128)} %get-tuple-element.73), channel_id=1, source_target_pairs={{0,1},{1,0},{2,3},{3,2},{4,5},{5,4},{6,7},{7,6},{8,9},{9,8},{10,11... | collective-permute-start | bytes 786440 | tf_op jit(solution)/shard_map/ppermute | solution.py:23
  195.1 8.0 %shard_map.109 = (bf16[512,2048]{1,0:T(8,128)(2,1)}, f32[2048,512]{1,0:T(8,128)}, f32[2048,512]{1,0:T(8,128)}, f32[1,16,128,128]{3,2,1,0:T(8,128)}, f32[16,8,512]{2,1,0:T(8,128)S(1)}) custom-call(s32[2]{0:T(128)S(1)} %copy-done.15, bf16[2048,512]{1,0:T(8,128)(2,1)S(1)} %copy-done.7, ...), custom_call_target="tpu_custom_call", output_to_operand_aliasing={{0}: (9, {}), {1}: (10, {}), {2}: (11, {}), {3}: (12, {}), ... | custom-call | flops 1879048192 | bytes 10485760 | tf_op jit(solution)/shard_map/pallas_call | solution.py:417
  203.1 6.4 %shard_map.110 = (bf16[512,2048]{1,0:T(8,128)(2,1)}, f32[2048,512]{1,0:T(8,128)}, f32[2048,512]{1,0:T(8,128)}, f32[1,16,128,128]{3,2,1,0:T(8,128)}, f32[16,8,512]{2,1,0:T(8,128)S(1)}) custom-call(s32[2]{0:T(128)S(1)} %copy-done.15, bf16[2048,512]{1,0:T(8,128)(2,1)S(1)} %copy-done.7, ...), custom_call_target="tpu_custom_call", output_to_operand_aliasing={{0}: (9, {}), {1}: (10, {}), {2}: (11, {}), {3}: (12, {}), ... | custom-call | flops 1409286144 | bytes 7864320 | tf_op jit(solution)/shard_map/pallas_call | solution.py:417
  211.4 2.1 collective-permute-done.10.refs_1_
  213.4 8.9 %shard_map.112 = (bf16[512,2048]{1,0:T(8,128)(2,1)}, bf16[512,2048]{1,0:T(8,128)(2,1)}) custom-call(s32[2]{0:T(128)} %pad_add_fusion.bits_ref, bf16[512,2048]{1,0:T(8,128)(2,1)} %bitcast.115, bf16[512,2048]{1,0:T(8,128)(2,1)} %bitcast.122, f32[2048,512]{1,0:T(8,128)} %get-tuple-element.53.gk_ref, f32[2048,512]{1,0:T(8,128)} %get-tuple-element.54.gv_ref, ...), custom_call_target="tpu_custom_call" | custom-call | flops 536870912 | bytes 16777216 | tf_op jit(solution)/shard_map/pallas_call | solution.py:435
  (87 shorter events, 38.7 us)
Async XLA Ops:
  0.6 22.9 %copy-start = (bf16[1,512,2048]{2,1,0:T(8,128)(2,1)S(1)}, bf16[1,512,2048]{2,1,0:T(8,128)(2,1)}, u32[]{:S(2)}) copy-start(bf16[1,512,2048]{2,1,0:T(8,128)(2,1)} %param.11) | copy-start | bytes 6291460
  0.6 24.7 %copy-start.19 = (f32[1,512,128]{2,1,0:T(8,128)S(1)}, f32[1,512,128]{2,1,0:T(8,128)}, u32[]{:S(2)}) copy-start(f32[1,512,128]{2,1,0:T(8,128)} %param.9) | copy-start | bytes 786436
  5.4 13.9 %collective-permute-start.7 = (bf16[16,128,128]{2,1,0:T(8,128)(2,1)}, bf16[16,128,128]{2,1,0:T(8,128)(2,1)S(1)}, u32[]{:S(2)}, u32[]{:S(2)}) collective-permute-start(bf16[16,128,128]{2,1,0:T(8,128)(2,1)} %get-tuple-element.41), channel_id=1, source_target_pairs={{0,8},{8,0},{16,24},{24,16},{1,9},{9,1},{17,25},{25,17},{2,10},{10... | collective-permute-start | bytes 1572872 | tf_op jit(solution)/shard_map/ppermute | solution.py:23
  21.3 25.3 %collective-permute-start.8 = (bf16[16,128,128]{2,1,0:T(8,128)(2,1)}, bf16[16,128,128]{2,1,0:T(8,128)(2,1)S(1)}, u32[]{:S(2)}, u32[]{:S(2)}) collective-permute-start(bf16[16,128,128]{2,1,0:T(8,128)(2,1)} %add_convert_fusion.1), channel_id=1, source_target_pairs={{0,16},{8,24},{16,0},{24,8},{1,17},{9,25},{17,1},{25,9},{2,18},{10... | collective-permute-start | bytes 1572872 | tf_op jit(solution)/shard_map/ppermute | solution.py:23
  23.5 32.2 %collective-permute-start.13 = (bf16[512,2048]{1,0:T(8,128)(2,1)S(1)}, bf16[512,2048]{1,0:T(8,128)(2,1)}, u32[]{:S(2)}, u32[]{:S(2)}) collective-permute-start(bf16[512,2048]{1,0:T(8,128)(2,1)S(1)} %bitcast.103), channel_id=1, source_target_pairs={{0,1},{1,0},{2,3},{3,2},{4,5},{5,4},{6,7},{7,6},{8,9},{9,8},{10,11... | collective-permute-start | bytes 6291464 | tf_op jit(solution)/shard_map/ppermute | solution.py:23
  46.6 7.7 %copy-start.11 = (bf16[16,128,128]{2,1,0:T(8,128)(2,1)}, bf16[16,128,128]{2,1,0:T(8,128)(2,1)S(1)}, u32[]{:S(2)}) copy-start(bf16[16,128,128]{2,1,0:T(8,128)(2,1)S(1)} %collective-permute-done.8.refs_1_) | copy-start | bytes 1572868
  54.3 5.5 %collective-permute-start.12 = (bf16[2048,512]{1,0:T(8,128)(2,1)}, bf16[2048,512]{1,0:T(8,128)(2,1)}, u32[]{:S(2)}, u32[]{:S(2)}) collective-permute-start(bf16[2048,512]{1,0:T(8,128)(2,1)} %shard_map.113.attn_ref), channel_id=1, source_target_pairs={{0,1},{1,0},{2,3},{3,2},{4,5},{5,4},{6,7},{7,6},{8,9},{9,8},{10,11... | collective-permute-start | bytes 6291464 | tf_op jit(solution)/shard_map/ppermute | solution.py:23
  65.7 24.7 %collective-permute-start.14 = (bf16[1024,512]{1,0:T(8,128)(2,1)}, bf16[1024,512]{1,0:T(8,128)(2,1)}, u32[]{:S(2)}, u32[]{:S(2)}) collective-permute-start(bf16[1024,512]{1,0:T(8,128)(2,1)} %get-tuple-element.64), channel_id=1, source_target_pairs={{0,2},{1,3},{2,0},{3,1},{4,6},{5,7},{6,4},{7,5},{8,10},{9,11},{10,... | collective-permute-start | bytes 3145736 | tf_op jit(solution)/shard_map/ppermute | solution.py:23
  66.8 32.1 %collective-permute-start.16 = (bf16[1024,512]{1,0:T(8,128)(2,1)}, bf16[1024,512]{1,0:T(8,128)(2,1)}, u32[]{:S(2)}, u32[]{:S(2)}) collective-permute-start(bf16[1024,512]{1,0:T(8,128)(2,1)} %get-tuple-element.66), channel_id=1, source_target_pairs={{0,4},{1,5},{2,6},{3,7},{4,0},{5,1},{6,2},{7,3},{8,12},{9,13},{10,... | collective-permute-start | bytes 3145736 | tf_op jit(solution)/shard_map/ppermute | solution.py:23
  68.0 45.6 %collective-permute-start.4 = (bf16[256,2048]{1,0:T(8,128)(2,1)}, bf16[256,2048]{1,0:T(8,128)(2,1)}, u32[]{:S(2)}, u32[]{:S(2)}) collective-permute-start(bf16[256,2048]{1,0:T(8,128)(2,1)} %refs_0_.1), channel_id=1, source_target_pairs={{0,4},{1,5},{2,6},{3,7},{4,0},{5,1},{6,2},{7,3},{8,12},{9,13},{10,... | collective-permute-start | bytes 3145736 | tf_op jit(solution)/shard_map/ppermute | solution.py:23
  68.3 45.8 %collective-permute-start.2 = (bf16[256,2048]{1,0:T(8,128)(2,1)}, bf16[256,2048]{1,0:T(8,128)(2,1)}, u32[]{:S(2)}, u32[]{:S(2)}) collective-permute-start(bf16[256,2048]{1,0:T(8,128)(2,1)} %refs_0_.1), channel_id=1, source_target_pairs={{0,2},{1,3},{2,0},{3,1},{4,6},{5,7},{6,4},{7,5},{8,10},{9,11},{10,... | collective-permute-start | bytes 3145736 | tf_op jit(solution)/shard_map/ppermute | solution.py:23
  68.6 70.5 %collective-permute-start = (bf16[256,2048]{1,0:T(8,128)(2,1)}, bf16[256,2048]{1,0:T(8,128)(2,1)}, u32[]{:S(2)}, u32[]{:S(2)}) collective-permute-start(bf16[256,2048]{1,0:T(8,128)(2,1)} %refs_0_.1), channel_id=1, source_target_pairs={{0,6},{1,7},{2,4},{3,5},{4,2},{5,3},{6,0},{7,1},{8,14},{9,15},{10,... | collective-permute-start | bytes 3145736 | tf_op jit(solution)/shard_map/ppermute | solution.py:23
  90.3 48.8 %collective-permute-start.6 = (bf16[256,2048]{1,0:T(8,128)(2,1)}, bf16[256,2048]{1,0:T(8,128)(2,1)S(1)}, u32[]{:S(2)}, u32[]{:S(2)}) collective-permute-start(bf16[256,2048]{1,0:T(8,128)(2,1)} %refs_0_.1), channel_id=1, source_target_pairs={{0,1},{1,0},{2,3},{3,2},{4,5},{5,4},{6,7},{7,6},{8,9},{9,8},{10,11... | collective-permute-start | bytes 3145736 | tf_op jit(solution)/shard_map/ppermute | solution.py:23
  98.8 49.1 %collective-permute-start.15 = (bf16[4,128,512]{2,1,0:T(8,128)(2,1)S(1)}, bf16[4,128,512]{2,1,0:T(8,128)(2,1)S(1)}, u32[]{:S(2)}, u32[]{:S(2)}) collective-permute-start(bf16[4,128,512]{2,1,0:T(8,128)(2,1)S(1)} %fusion.9), channel_id=1, source_target_pairs={{0,4},{1,5},{2,6},{3,7},{4,0},{5,1},{6,2},{7,3},{8,12},{9,13},{10,... | collective-permute-start | bytes 1572872 | tf_op jit(solution)/shard_map/ppermute | solution.py:23
  113.6 35.6 %collective-permute-start.17 = (bf16[4,128,512]{2,1,0:T(8,128)(2,1)S(1)}, bf16[4,128,512]{2,1,0:T(8,128)(2,1)S(1)}, u32[]{:S(2)}, u32[]{:S(2)}) collective-permute-start(bf16[4,128,512]{2,1,0:T(8,128)(2,1)S(1)} %fusion.10), channel_id=1, source_target_pairs={{0,2},{1,3},{2,0},{3,1},{4,6},{5,7},{6,4},{7,5},{8,10},{9,11},{10,... | collective-permute-start | bytes 1572872 | tf_op jit(solution)/shard_map/ppermute | solution.py:23
  114.1 38.4 %collective-permute-start.5 = (bf16[256,2048]{1,0:T(8,128)(2,1)}, bf16[256,2048]{1,0:T(8,128)(2,1)S(1)}, u32[]{:S(2)}, u32[]{:S(2)}) collective-permute-start(bf16[256,2048]{1,0:T(8,128)(2,1)} %collective-permute-done.4.refs_1_), channel_id=1, source_target_pairs={{0,1},{1,0},{2,3},{3,2},{4,5},{5,4},{6,7},{7,6},{8,9},{9,8},{10,11... | collective-permute-start | bytes 3145736 | tf_op jit(solution)/shard_map/ppermute | solution.py:23
  139.1 13.3 %collective-permute-start.3 = (bf16[256,2048]{1,0:T(8,128)(2,1)}, bf16[256,2048]{1,0:T(8,128)(2,1)S(1)}, u32[]{:S(2)}, u32[]{:S(2)}) collective-permute-start(bf16[256,2048]{1,0:T(8,128)(2,1)} %collective-permute-done.2.refs_0_), channel_id=1, source_target_pairs={{0,1},{1,0},{2,3},{3,2},{4,5},{5,4},{6,7},{7,6},{8,9},{9,8},{10,11... | collective-permute-start | bytes 3145736 | tf_op jit(solution)/shard_map/ppermute | solution.py:23
  139.2 16.0 %collective-permute-start.1 = (bf16[256,2048]{1,0:T(8,128)(2,1)}, bf16[256,2048]{1,0:T(8,128)(2,1)S(1)}, u32[]{:S(2)}, u32[]{:S(2)}) collective-permute-start(bf16[256,2048]{1,0:T(8,128)(2,1)} %collective-permute-done.refs_0_), channel_id=1, source_target_pairs={{0,1},{1,0},{2,3},{3,2},{4,5},{5,4},{6,7},{7,6},{8,9},{9,8},{10,11... | collective-permute-start | bytes 3145736 | tf_op jit(solution)/shard_map/ppermute | solution.py:23
  151.7 23.5 %collective-permute-start.18 = (bf16[2,128,1024]{2,1,0:T(8,128)(2,1)}, bf16[2,128,1024]{2,1,0:T(8,128)(2,1)}, u32[]{:S(2)}, u32[]{:S(2)}) collective-permute-start(bf16[2,128,1024]{2,1,0:T(8,128)(2,1)} %fusion.11), channel_id=1, source_target_pairs={{0,8},{8,0},{16,24},{24,16},{1,9},{9,1},{17,25},{25,17},{2,10},{10... | collective-permute-start | bytes 1572872 | tf_op jit(solution)/shard_map/ppermute | solution.py:23
  155.2 4.3 %copy-start.6 = (bf16[4096,512]{1,0:T(8,128)(2,1)S(1)}, bf16[4096,512]{1,0:T(8,128)(2,1)}, u32[]{:S(2)}) copy-start(bf16[4096,512]{1,0:T(8,128)(2,1)} %get-tuple-element.56.wq_ref) | copy-start | bytes 12582916
  161.1 5.2 %copy-start.2 = (bf16[2048,512]{1,0:T(8,128)(2,1)S(1)}, bf16[2048,512]{1,0:T(8,128)(2,1)}, u32[]{:S(2)}) copy-start(bf16[2048,512]{1,0:T(8,128)(2,1)} %shard_map.107.g_ref) | copy-start | bytes 6291460
  161.1 5.2 %copy-start.9 = (bf16[1,16,128,128]{3,2,1,0:T(8,128)(2,1)S(1)}, bf16[1,16,128,128]{3,2,1,0:T(8,128)(2,1)}, u32[]{:S(2)}) copy-start(bf16[1,16,128,128]{3,2,1,0:T(8,128)(2,1)} %get-tuple-element.36.block_ref) | copy-start | bytes 1572868
  161.1 5.2 %copy-start.10 = (f32[1,512,128]{1,2,0:T(8,128)S(1)}, f32[1,512,128]{1,2,0:T(8,128)}, u32[]{:S(2)}) copy-start(f32[1,512,128]{1,2,0:T(8,128)} %copy.35) | copy-start | bytes 786436
  161.1 5.2 %copy-start.15 = (s32[2]{0:T(128)S(1)}, s32[2]{0:T(128)}, u32[]{:S(2)}) copy-start(s32[2]{0:T(128)} %pad_add_fusion.bits_ref) | copy-start | bytes 28
  164.8 14.8 %collective-permute-start.9 = (bf16[16,128,128]{2,1,0:T(8,128)(2,1)}, bf16[16,128,128]{2,1,0:T(8,128)(2,1)}, u32[]{:S(2)}, u32[]{:S(2)}) collective-permute-start(bf16[16,128,128]{2,1,0:T(8,128)(2,1)} %get-tuple-element.57), channel_id=1, source_target_pairs={{8,0},{24,16},{9,1},{25,17},{10,2},{26,18},{11,3},{27,19},{12,4},{... | collective-permute-start | bytes 1572872 | tf_op jit(solution)/shard_map/ppermute | solution.py:388
  172.1 3.1 %copy-start.17 = (f32[4,128,1024]{2,1,0:T(8,128)S(1)}, f32[4,128,1024]{2,1,0:T(8,128)}, u32[]{:S(2)}) copy-start(f32[4,128,1024]{2,1,0:T(8,128)} %copy-done.16) | copy-start | bytes 6291460
  172.1 7.5 %copy-start.14 = (f32[16,128,128]{2,1,0:T(8,128)S(1)}, f32[16,128,128]{2,1,0:T(8,128)}, u32[]{:S(2)}) copy-start(f32[16,128,128]{2,1,0:T(8,128)} %copy-done.13) | copy-start | bytes 3145732
  176.2 14.6 %collective-permute-start.19 = (bf16[128,1024]{1,0:T(8,128)(2,1)S(1)}, bf16[128,1024]{1,0:T(8,128)(2,1)S(1)}, u32[]{:S(2)}, u32[]{:S(2)}) collective-permute-start(bf16[128,1024]{1,0:T(8,128)(2,1)S(1)} %fusion.13), channel_id=1, source_target_pairs={{0,16},{8,24},{16,0},{24,8},{1,17},{9,25},{17,1},{25,9},{2,18},{10... | collective-permute-start | bytes 786440 | tf_op jit(solution)/shard_map/ppermute | solution.py:23
  181.6 29.8 %collective-permute-start.11 = (bf16[16,128,128]{2,1,0:T(8,128)(2,1)}, bf16[16,128,128]{2,1,0:T(8,128)(2,1)}, u32[]{:S(2)}, u32[]{:S(2)}) collective-permute-start(bf16[16,128,128]{2,1,0:T(8,128)(2,1)} %add_convert_fusion), channel_id=1, source_target_pairs={{16,8},{24,16},{17,9},{25,17},{18,10},{26,18},{19,11},{27,19},{20,... | collective-permute-start | bytes 1572872 | tf_op jit(solution)/shard_map/ppermute | solution.py:390
  183.1 30.3 %collective-permute-start.10 = (bf16[16,128,128]{2,1,0:T(8,128)(2,1)}, bf16[16,128,128]{2,1,0:T(8,128)(2,1)}, u32[]{:S(2)}, u32[]{:S(2)}) collective-permute-start(bf16[16,128,128]{2,1,0:T(8,128)(2,1)} %add_convert_fusion), channel_id=1, source_target_pairs={{16,0},{17,1},{18,2},{19,3},{20,4},{21,5},{22,6},{23,7}} | collective-permute-start | bytes 1572872 | tf_op jit(solution)/shard_map/ppermute | solution.py:390
  192.8 29.5 %collective-permute-start.20 = (f32[64,1024]{1,0:T(8,128)}, f32[64,1024]{1,0:T(8,128)}, u32[]{:S(2)}, u32[]{:S(2)}) collective-permute-start(f32[64,1024]{1,0:T(8,128)} %get-tuple-element.73), channel_id=1, source_target_pairs={{0,1},{1,0},{2,3},{3,2},{4,5},{5,4},{6,7},{7,6},{8,9},{9,8},{10,11... | collective-permute-start | bytes 786440 | tf_op jit(solution)/shard_map/ppermute | solution.py:23
  213.4 8.9 %copy-start.18 = (f32[64,1024]{1,0:T(8,128)S(1)}, f32[64,1024]{1,0:T(8,128)}, u32[]{:S(2)}) copy-start(f32[64,1024]{1,0:T(8,128)} %get-tuple-element.72) | copy-start | bytes 786436
  (9 other events, 14.7 us)
